TPU v7x, 512 devices: a whole 4x8x8 slice. The times are simulated.
512 devices in a mesh: lon: 128 (over z_hi, x, y, core), lev: 4 (over z_lo).
Axes of the slice: x: 4, y: 8, z: 8 (z_hi: 2, z_lo: 4; z = z_hi * 4 + z_lo), core: 2. Of those that a mesh axis runs over, the one named last changes fastest.
Arguments:
- thickness: float32 [4, 2048, 2048], P('lev', 'lon'), may hold values from 0.5 to 1.5
- wind_field: float32 [2, 4, 2048, 2048], P(None, 'lev', 'lon'), may hold values from -3 to 3
Outputs:
- new_thickness: float32 [4, 2048, 2048], P('lev', 'lon')
- new_winds: float32 [2, 4, 2048, 2048], P(None, 'lev', 'lon')
All inputs are finite; a program needn't handle non-finite values.
Results may differ from a plain program's by a relative error of at most 0.0001.
Values sent between devices are 32-bit elements; how exact they have to be, the bound alone decides.
A program may use at most 64 MiB of HBM per device.

v0:
```python
import math

import jax
import jax.numpy as jnp
from jax import lax
from jax.sharding import PartitionSpec as P

STEPS = 2


courant = 0.2
mixing = 0.25
coriolis = 0.5
cos_floor = 0.25
highest = lax.Precision.HIGHEST


def with_halo(value, sides, width, wrap):
    for axis, dim in sides:
        size, length = (lax.axis_size(axis), value.shape[dim])
        up = [(i, (i + 1) % size) for i in range(size if wrap else size - 1)]
        down = [(j, i) for i, j in up]
        last = lax.slice_in_dim(value, length - width, length, axis=dim)
        initial = lax.slice_in_dim(value, 0, width, axis=dim)
        before = lax.ppermute(last, axis, up)
        after = lax.ppermute(initial, axis, down)
        value = jnp.concatenate([before, value, after], axis=dim)
    return value


def from_partner(value, axis, bit):
    return lax.ppermute(value, axis, [(i, i ^ 1 << bit) for i in range(lax.axis_size(axis))])


def angle_tables(count_first, count_second, modulus):
    products = (
        jnp.arange(count_first, dtype=jnp.int32)[:, None]
        * jnp.arange(count_second, dtype=jnp.int32)[None, :]
        % modulus
    )
    angles = products.astype(jnp.float32) * (2.0 * math.pi / modulus)
    return (jnp.cos(angles), jnp.sin(angles))


def small_product(table, values):
    return jnp.einsum(
        "kn,bnp->bkp", table, values, precision=highest, preferred_element_type=jnp.float32
    )


def circle_transform(circles, kept_blocks):
    batch_size, length = circles.shape
    radix_size = 128
    blocks = length // radix_size
    cos_small, sin_small = angle_tables(blocks, blocks, blocks)
    cos_twist, sin_twist = angle_tables(blocks, radix_size, length)
    cos_radix, sin_radix = angle_tables(radix_size, radix_size, radix_size)
    shaped = circles.reshape(batch_size, blocks, radix_size)
    first_real = small_product(cos_small, shaped)
    first_imag = -small_product(sin_small, shaped)
    twist_real = first_real * cos_twist + first_imag * sin_twist
    twist_imag = first_imag * cos_twist - first_real * sin_twist
    forward_table = jnp.concatenate(
        [jnp.concatenate([cos_radix, -sin_radix], 1), jnp.concatenate([sin_radix, cos_radix], 1)], 0
    )
    joined = jnp.concatenate([twist_real, twist_imag], 2).reshape(
        batch_size * blocks, 2 * radix_size
    )
    spectrum = jnp.dot(joined, forward_table, precision=highest, preferred_element_type=jnp.float32)
    index_grid = (
        blocks * jnp.arange(radix_size, dtype=jnp.int32)[None, :]
        + jnp.arange(blocks, dtype=jnp.int32)[:, None]
    )
    signed = jnp.where(index_grid > length // 2, index_grid - length, index_grid)
    retained = (jnp.abs(signed) <= length // 3).astype(jnp.float32)
    factor = retained * (1.0 - 2.0 * math.pi / length * signed.astype(jnp.float32)) / length
    factor_pair = jnp.concatenate([factor, factor], 1)
    weighted = spectrum.reshape(batch_size, blocks, 2 * radix_size) * factor_pair
    inverse_table = jnp.concatenate(
        [jnp.concatenate([cos_radix, sin_radix], 1), jnp.concatenate([-sin_radix, cos_radix], 1)], 0
    )
    inverse_first = jnp.dot(
        weighted.reshape(batch_size * blocks, 2 * radix_size),
        inverse_table,
        precision=highest,
        preferred_element_type=jnp.float32,
    )
    inverse_first = inverse_first.reshape(batch_size, blocks, 2 * radix_size)
    first_half = inverse_first[:, :, :radix_size]
    second_half = inverse_first[:, :, radix_size:]
    turn_real = first_half * cos_twist - second_half * sin_twist
    turn_imag = first_half * sin_twist + second_half * cos_twist
    cos_rows = cos_small[:kept_blocks]
    sin_rows = sin_small[:kept_blocks]
    out_real = small_product(cos_rows, turn_real) - small_product(sin_rows, turn_imag)
    out_imag = small_product(sin_rows, turn_real) + small_product(cos_rows, turn_imag)
    return (
        out_real.reshape(batch_size, kept_blocks * radix_size),
        out_imag.reshape(batch_size, kept_blocks * radix_size),
    )


def body(thickness, wind_field):
    fields_now = jnp.concatenate([thickness[None], wind_field], 0)
    level_count, lon_count, lat_count = thickness.shape
    circle_blocks = 2 * lat_count // 128
    latitude = (jnp.arange(lat_count).astype(jnp.float32) + 0.5) * (
        math.pi / lat_count
    ) - 0.5 * math.pi
    secant = 1.0 / jnp.maximum(jnp.cos(latitude), cos_floor)
    coriolis_term = coriolis * jnp.sin(latitude)
    sign_column = jnp.array([1.0, -1.0, -1.0], jnp.float32).reshape(3, 1, 1, 1)
    partner_bit = lax.axis_size("lon").bit_length() - 2
    for step_index in range(STEPS):
        widened = with_halo(fields_now, (("lon", 2),), 3, True)
        zonal_slope = (
            45.0 * (widened[:, :, 4 : lon_count + 4] - widened[:, :, 2 : lon_count + 2])
            - 9.0 * (widened[:, :, 5 : lon_count + 5] - widened[:, :, 1 : lon_count + 1])
            + (widened[:, :, 6 : lon_count + 6] - widened[:, :, 0:lon_count])
        ) / 60.0
        stacked_levels = with_halo(fields_now[0], (("lev", 0),), 1, False)
        vertical = stacked_levels[2:] + stacked_levels[:-2] - 2.0 * fields_now[0]
        antipode = from_partner(fields_now, "lon", partner_bit)
        circle = jnp.concatenate([fields_now, sign_column * antipode[..., ::-1]], 3).reshape(
            -1, 2 * lat_count
        )
        smooth_flat, slope_flat = circle_transform(circle, circle_blocks // 2)
        smooth = smooth_flat.reshape(fields_now.shape)
        meridional_slope = slope_flat.reshape(fields_now.shape)
        thickness_now = fields_now[0]
        eastward = fields_now[1]
        northward = fields_now[2]
        advect = eastward * secant * zonal_slope + northward * meridional_slope
        height_tendency = (
            -advect[0]
            - thickness_now * (secant * zonal_slope[1] + meridional_slope[2])
            + mixing * vertical
        )
        east_tendency = -advect[1] - secant * zonal_slope[0] + coriolis_term * northward
        north_tendency = -advect[2] - meridional_slope[0] - coriolis_term * eastward
        fields_now = smooth + courant * jnp.stack([height_tendency, east_tendency, north_tendency])
    return (fields_now[0], fields_now[1:])


def solution(mesh):
    in_specs = (P("lev", "lon", None), P(None, "lev", "lon", None))
    out_specs = (P("lev", "lon", None), P(None, "lev", "lon", None))
    return jax.shard_map(body, mesh=mesh, in_specs=in_specs, out_specs=out_specs, check_vma=False)
```

profile of v0, /device:TPU:64, one launch (start us, length us, event | category | flops | bytes accessed | tf_op | source)
XLA Modules:
  0.0 108.9 jit_solution(6897552432452379239)
XLA Ops:
  0.7 7.0 %collective-permute-start.3 = (f32[1,16,2048]{2,1,0:T(8,128)}, f32[1,16,2048]{2,1,0:T(8,128)}, u32[]{:S(2)}, u32[]{:S(2)}) collective-permute-start(f32[1,16,2048]{2,1,0:T(8,128)} %param.3), channel_id=1, source_target_pairs={{1,0},{2,1},{3,2},{5,4},{6,5},{7,6},{9,8},{10,9},{11,10},{13,12},{... | collective-permute-start | bytes 393224 | tf_op jit(solution)/shard_map/ppermute | solution.py:26
  7.7 1.9 %collective-permute-start.4 = (f32[1,16,2048]{2,1,0:T(8,128)}, f32[1,16,2048]{2,1,0:T(8,128)}, u32[]{:S(2)}, u32[]{:S(2)}) collective-permute-start(f32[1,16,2048]{2,1,0:T(8,128)} %param.3), channel_id=1, source_target_pairs={{0,1},{1,2},{2,3},{4,5},{5,6},{6,7},{8,9},{9,10},{10,11},{12,13},{... | collective-permute-start | bytes 393224 | tf_op jit(solution)/shard_map/ppermute | solution.py:25
  9.6 1.0 pad_maximum_fusion.2
  10.7 7.0 %collective-permute-start = (f32[3,1,16,2048]{3,2,1,0:T(8,128)S(1)}, f32[3,1,16,2048]{3,2,1,0:T(8,128)S(1)}, u32[]{:S(2)}, u32[]{:S(2)}) collective-permute-start(f32[3,1,16,2048]{3,2,1,0:T(8,128)S(1)} %pad_maximum_fusion.2), channel_id=1, source_target_pairs={{0,256},{4,260},{8,264},{12,268},{16,272},{20,276},{24,280},{28,28... | collective-permute-start | bytes 1179656 | tf_op jit(solution)/shard_map/ppermute | solution.py:32
  17.7 1.0 fusion.73
  18.8 5.9 %collective-permute-start.1 = (f32[3,1,3,2048]{3,2,1,0:T(4,128)S(1)}, f32[3,1,3,2048]{3,2,1,0:T(4,128)S(1)}, u32[]{:S(2)}, u32[]{:S(2)}) collective-permute-start(f32[3,1,3,2048]{3,2,1,0:T(4,128)S(1)} %get-tuple-element.25), channel_id=1, source_target_pairs={{4,0},{8,4},{12,8},{16,12},{20,16},{24,20},{28,24},{32,28},{36,32}... | collective-permute-start | bytes 221192 | tf_op jit(solution)/shard_map/ppermute | solution.py:26
  24.7 1.9 %collective-permute-start.2 = (f32[3,1,3,2048]{3,2,1,0:T(4,128)S(1)}, f32[3,1,3,2048]{3,2,1,0:T(4,128)S(1)}, u32[]{:S(2)}, u32[]{:S(2)}) collective-permute-start(f32[3,1,3,2048]{3,2,1,0:T(4,128)S(1)} %get-tuple-element.26), channel_id=1, source_target_pairs={{0,4},{4,8},{8,12},{12,16},{16,20},{20,24},{24,28},{28,32},{32,36}... | collective-permute-start | bytes 221192 | tf_op jit(solution)/shard_map/ppermute | solution.py:25
  27.4 0.7 multiply_bitcast_fusion.1
  28.3 10.8 %collective-permute-done.2 = f32[3,1,3,2048]{3,2,1,0:T(4,128)S(1)} collective-permute-done((f32[3,1,3,2048]{3,2,1,0:T(4,128)S(1)}, f32[3,1,3,2048]{3,2,1,0:T(4,128)S(1)}, u32[]{:S(2)}, u32[]{:S(2)}) %collective-permute-start.2) | collective-permute-done | bytes 73760 | tf_op jit(solution)/shard_map/ppermute | solution.py:25
  39.2 1.0 broadcast_multiply_fusion.1
  40.2 1.2 %rev.6 = f32[3,1,16,2048]{3,2,1,0:T(8,128)S(1)} reverse(f32[3,1,16,2048]{3,2,1,0:T(8,128)S(1)} %collective-permute-done), dimensions={3} | reverse | bytes 786432 | tf_op jit(solution)/shard_map/rev | solution.py:124
  41.8 0.9 convolution_bitcast_fusion.1
  42.6 1.0 multiply_add_fusion.3
  43.7 1.4 %fusion = f32[48,32,256]{2,1,0:T(8,128)S(1)} fusion(f32[48,32,128]{2,1,0:T(8,128)S(1)} %get-tuple-element.9, f32[48,32,128]{2,1,0:T(8,128)S(1)} %get-tuple-element.8, f32[128,128]{1,0:T(8,128)S(1)} %get-tuple-element.32, f32[128,128]{1,0:T(8,128)S(1)} %get-tuple-element.31, f32[128,128]{1,0:T(8,128)S(1)} %fusion.83), kind=kOutput, calls=%fused_computation | convolution fusion | flops 1208549376 | bytes 3342336 | tf_op jit(solution)/shard_map/dot_general | solution.py:69
  45.1 1.4 %fusion.10 = f32[48,32,256]{2,1,0:T(8,128)S(1)} fusion(f32[48,32,256]{2,1,0:T(8,128)S(1)} %fusion, f32[32,256]{1,0:T(8,128)S(1)} %pad_maximum_fusion.10, f32[128,128]{1,0:T(8,128)S(1)} %get-tuple-element.32, f32[128,128]{1,0:T(8,128)S(1)} %fusion.83, f32[128,128]{1,0:T(8,128)S(1)} %get-tuple-element.31), kind=kOutput, calls=%fused_computation.10 | convolution fusion | flops 1208549376 | bytes 3375104 | tf_op jit(solution)/shard_map/dot_general | solution.py:82
  46.5 1.4 %fusion.48 = f32[48,128,16]{1,2,0:T(8,128)} fusion(f32[48,32,256]{2,1,0:T(8,128)S(1)} %fusion.10, f32[32,128]{1,0:T(8,128)S(1)} %get-tuple-element.29, f32[32,128]{1,0:T(8,128)S(1)} %get-tuple-element.30, f32[32,32]{1,0:T(8,128)S(1)} %fusion.103), kind=kOutput, calls=%fused_computation.94 | convolution fusion | flops 38338560 | bytes 2007040 | tf_op jit(solution)/shard_map/kn,bnp->bkp/dot_general | solution.py:46
  48.5 0.6 fusion.16
  49.2 0.7 fusion.132
  49.9 1.6 %squeeze.18 = f32[1,1,16,2048]{3,2,1,0:T(8,128)} reshape(f32[16,16,128]{2,1,0:T(8,128)} %get-tuple-element.22) | data formatting | bytes 262144 | tf_op jit(solution)/shard_map/squeeze | solution.py:140
  51.5 1.1 fusion.38
  52.5 1.0 fusion.65
  53.6 1.3 %fusion.17 = f32[48,16,128]{2,1,0:T(8,128)S(1)} fusion(f32[48,128,16]{1,2,0:T(8,128)S(1)} %copy-done.4, f32[48,32,256]{2,1,0:T(8,128)S(1)} %fusion.10, f32[32,128]{1,0:T(8,128)S(1)} %get-tuple-element.29, f32[32,128]{1,0:T(8,128)S(1)} %get-tuple-element.30, f32[32,32]{1,0:T(8,128)} %copy-done.5), kind=kOutput, calls=%fused_computation.25 | convolution fusion | flops 38436864 | bytes 2400256 | tf_op jit(solution)/shard_map/kn,bnp->bkp/dot_general | solution.py:46
  55.0 1.1 fusion.71
  56.2 7.6 %collective-permute-start.5 = (f32[3,1,16,2048]{3,2,1,0:T(8,128)S(1)}, f32[3,1,16,2048]{3,2,1,0:T(8,128)S(1)}, u32[]{:S(2)}, u32[]{:S(2)}) collective-permute-start(f32[3,1,16,2048]{3,2,1,0:T(8,128)S(1)} %fusion.35), channel_id=1, source_target_pairs={{0,256},{4,260},{8,264},{12,268},{16,272},{20,276},{24,280},{28,28... | collective-permute-start | bytes 1179656 | tf_op jit(solution)/shard_map/ppermute | solution.py:32
  63.9 1.9 %collective-permute-start.6 = (f32[3,1,3,2048]{3,2,1,0:T(4,128)S(1)}, f32[3,1,3,2048]{3,2,1,0:T(4,128)S(1)}, u32[]{:S(2)}, u32[]{:S(2)}) collective-permute-start(f32[3,1,3,2048]{3,2,1,0:T(4,128)S(1)} %get-tuple-element.19), channel_id=1, source_target_pairs={{4,0},{8,4},{12,8},{16,12},{20,16},{24,20},{28,24},{32,28},{36,32}... | collective-permute-start | bytes 221192 | tf_op jit(solution)/shard_map/ppermute | solution.py:26
  65.8 2.6 %collective-permute-start.7 = (f32[3,1,3,2048]{3,2,1,0:T(4,128)S(1)}, f32[3,1,3,2048]{3,2,1,0:T(4,128)S(1)}, u32[]{:S(2)}, u32[]{:S(2)}) collective-permute-start(f32[3,1,3,2048]{3,2,1,0:T(4,128)S(1)} %get-tuple-element.20), channel_id=1, source_target_pairs={{0,4},{4,8},{8,12},{12,16},{16,20},{20,24},{24,28},{28,32},{32,36}... | collective-permute-start | bytes 221192 | tf_op jit(solution)/shard_map/ppermute | solution.py:25
  68.4 0.7 multiply_bitcast_fusion
  69.1 11.0 %collective-permute-done.7 = f32[3,1,3,2048]{3,2,1,0:T(4,128)S(1)} collective-permute-done((f32[3,1,3,2048]{3,2,1,0:T(4,128)S(1)}, f32[3,1,3,2048]{3,2,1,0:T(4,128)S(1)}, u32[]{:S(2)}, u32[]{:S(2)}) %collective-permute-start.7) | collective-permute-done | bytes 73760 | tf_op jit(solution)/shard_map/ppermute | solution.py:25
  80.1 1.1 %broadcast_multiply_fusion = (f32[3,1,16,2048]{3,2,1,0:T(8,128)}, f32[3,1,16,2048]{3,2,1,0:T(8,128)S(1)}) fusion(f32[3,1,16,2048]{3,2,1,0:T(8,128)S(1)} %fusion.35, f32[3,1,3,2048]{3,2,1,0:T(4,128)S(1)} %collective-permute-done.7, f32[3,1,3,2048]{3,2,1,0:T(4,128)S(1)} %collective-permute-done.6), kind=kLoop, calls=%fused_computation.89 | loop fusion | flops 1376256 | bytes 1327104 | tf_op jit(solution)/shard_map/div | solution.py:116
  81.3 1.2 %rev.7 = f32[3,1,16,2048]{3,2,1,0:T(8,128)S(1)} reverse(f32[3,1,16,2048]{3,2,1,0:T(8,128)S(1)} %collective-permute-done.5), dimensions={3} | reverse | bytes 786432 | tf_op jit(solution)/shard_map/rev | solution.py:124
  82.8 0.9 convolution_bitcast_fusion
  83.7 1.0 multiply_add_fusion.1
  84.7 1.4 %fusion.4 = f32[48,32,256]{2,1,0:T(8,128)S(1)} fusion(f32[48,32,128]{2,1,0:T(8,128)S(1)} %get-tuple-element.7, f32[48,32,128]{2,1,0:T(8,128)S(1)} %get-tuple-element.6, f32[128,128]{1,0:T(8,128)S(1)} %get-tuple-element.32, f32[128,128]{1,0:T(8,128)S(1)} %get-tuple-element.31, f32[128,128]{1,0:T(8,128)S(1)} %fusion.83), kind=kOutput, calls=%fused_computation.4 | convolution fusion | flops 1208549376 | bytes 3342336 | tf_op jit(solution)/shard_map/dot_general | solution.py:69
  86.1 1.4 %fusion.8 = f32[48,32,256]{2,1,0:T(8,128)S(1)} fusion(f32[48,32,256]{2,1,0:T(8,128)S(1)} %fusion.4, f32[32,256]{1,0:T(8,128)S(1)} %pad_maximum_fusion.10, f32[128,128]{1,0:T(8,128)S(1)} %get-tuple-element.32, f32[128,128]{1,0:T(8,128)S(1)} %fusion.83, f32[128,128]{1,0:T(8,128)S(1)} %get-tuple-element.31), kind=kOutput, calls=%fused_computation.8 | convolution fusion | flops 1208549376 | bytes 3375104 | tf_op jit(solution)/shard_map/dot_general | solution.py:82
  87.6 1.4 %fusion.50 = f32[48,128,16]{1,2,0:T(8,128)} fusion(f32[48,32,256]{2,1,0:T(8,128)S(1)} %fusion.8, f32[32,128]{1,0:T(8,128)S(1)} %get-tuple-element.29, f32[32,128]{1,0:T(8,128)S(1)} %get-tuple-element.30, f32[32,32]{1,0:T(8,128)S(1)} %copy-done.8), kind=kOutput, calls=%fused_computation.96 | convolution fusion | flops 38338560 | bytes 2007040 | tf_op jit(solution)/shard_map/kn,bnp->bkp/dot_general | solution.py:46
  89.6 0.6 fusion.14
  90.3 0.7 fusion.130
  91.0 1.1 fusion.37
  92.1 1.8 %fusion.54 = (f32[1,1,16,2048]{3,2,1,0:T(8,128)}, f32[1,1,16,2048]{3,2,1,0:T(8,128)}, f32[1,16,2048]{2,1,0:T(8,128)}) fusion(f32[3,1,16,2048]{3,2,1,0:T(8,128)} %get-tuple-element.2, f32[3,1,16,2048]{3,2,1,0:T(8,128)S(1)} %fusion.37, f32[3,1,16,2048]{3,2,1,0:T(8,128)S(1)} %fusion.35, f32[2048]{0:T(1024)S(1)} %get-tuple-element.33, ...), kind=kLoop, calls=%fused_computation.103 | loop fusion | flops 294912 | bytes 1327104 | tf_op jit(solution)/shard_map/add | solution.py:139
  93.9 4.3 %collective-permute-start.8 = (f32[1,16,2048]{2,1,0:T(8,128)}, f32[1,16,2048]{2,1,0:T(8,128)}, u32[]{:S(2)}, u32[]{:S(2)}) collective-permute-start(f32[1,16,2048]{2,1,0:T(8,128)} %get-tuple-element.14), channel_id=1, source_target_pairs={{1,0},{2,1},{3,2},{5,4},{6,5},{7,6},{9,8},{10,9},{11,10},{13,12},{... | collective-permute-start | bytes 393224 | tf_op jit(solution)/shard_map/ppermute | solution.py:26
  98.2 2.4 %collective-permute-start.9 = (f32[1,16,2048]{2,1,0:T(8,128)}, f32[1,16,2048]{2,1,0:T(8,128)}, u32[]{:S(2)}, u32[]{:S(2)}) collective-permute-start(f32[1,16,2048]{2,1,0:T(8,128)} %get-tuple-element.14), channel_id=1, source_target_pairs={{0,1},{1,2},{2,3},{4,5},{5,6},{6,7},{8,9},{9,10},{10,11},{12,13},{... | collective-permute-start | bytes 393224 | tf_op jit(solution)/shard_map/ppermute | solution.py:25
  100.7 0.6 fusion.15
  101.4 0.9 squeeze.21
  102.3 3.1 %collective-permute-done.9 = f32[1,16,2048]{2,1,0:T(8,128)} collective-permute-done((f32[1,16,2048]{2,1,0:T(8,128)}, f32[1,16,2048]{2,1,0:T(8,128)}, u32[]{:S(2)}, u32[]{:S(2)}) %collective-permute-start.9) | collective-permute-done | bytes 131104 | tf_op jit(solution)/shard_map/ppermute | solution.py:25
  105.4 1.1 %fusion.60 = f32[1,1,16,2048]{3,2,1,0:T(8,128)S(1)} fusion(f32[1,16,2048]{2,1,0:T(8,128)S(1)} %squeeze.21, f32[3,1,16,2048]{3,2,1,0:T(8,128)} %get-tuple-element.2, f32[3,1,16,2048]{3,2,1,0:T(8,128)} %copy-done.2, f32[1,16,2048]{2,1,0:T(8,128)} %collective-permute-done.8, f32[1,16,2048]{2,1,0:T(8,128)} %collective-permute-done.9, ...), kind=kLoop, calls=%fused_computation.111 | loop fusion | flops 327680 | bytes 925696 | tf_op jit(solution)/shard_map/stack | solution.py:141
  106.5 1.0 fusion.36
  107.6 0.7 slice.248
  108.3 0.7 slice_bitcast_fusion
  (55 shorter events, 3.3 us)
Async XLA Ops:
  0.6 38.5 %copy-start.1 = (f32[1,16,2048]{2,1,0:T(8,128)S(1)}, f32[1,16,2048]{2,1,0:T(8,128)}, u32[]{:S(2)}) copy-start(f32[1,16,2048]{2,1,0:T(8,128)} %param.3) | copy-start | bytes 393220
  0.6 26.8 %copy-start = (f32[2,1,16,2048]{3,2,1,0:T(8,128)S(1)}, f32[2,1,16,2048]{3,2,1,0:T(8,128)}, u32[]{:S(2)}) copy-start(f32[2,1,16,2048]{3,2,1,0:T(8,128)} %param.4) | copy-start | bytes 786436
  0.7 54.3 %collective-permute-start.3 = (f32[1,16,2048]{2,1,0:T(8,128)}, f32[1,16,2048]{2,1,0:T(8,128)}, u32[]{:S(2)}, u32[]{:S(2)}) collective-permute-start(f32[1,16,2048]{2,1,0:T(8,128)} %param.3), channel_id=1, source_target_pairs={{1,0},{2,1},{3,2},{5,4},{6,5},{7,6},{9,8},{10,9},{11,10},{13,12},{... | collective-permute-start | bytes 393224 | tf_op jit(solution)/shard_map/ppermute | solution.py:26
  7.7 47.3 %collective-permute-start.4 = (f32[1,16,2048]{2,1,0:T(8,128)}, f32[1,16,2048]{2,1,0:T(8,128)}, u32[]{:S(2)}, u32[]{:S(2)}) collective-permute-start(f32[1,16,2048]{2,1,0:T(8,128)} %param.3), channel_id=1, source_target_pairs={{0,1},{1,2},{2,3},{4,5},{5,6},{6,7},{8,9},{9,10},{10,11},{12,13},{... | collective-permute-start | bytes 393224 | tf_op jit(solution)/shard_map/ppermute | solution.py:25
  10.7 29.5 %collective-permute-start = (f32[3,1,16,2048]{3,2,1,0:T(8,128)S(1)}, f32[3,1,16,2048]{3,2,1,0:T(8,128)S(1)}, u32[]{:S(2)}, u32[]{:S(2)}) collective-permute-start(f32[3,1,16,2048]{3,2,1,0:T(8,128)S(1)} %pad_maximum_fusion.2), channel_id=1, source_target_pairs={{0,256},{4,260},{8,264},{12,268},{16,272},{20,276},{24,280},{28,28... | collective-permute-start | bytes 1179656 | tf_op jit(solution)/shard_map/ppermute | solution.py:32
  18.8 9.5 %collective-permute-start.1 = (f32[3,1,3,2048]{3,2,1,0:T(4,128)S(1)}, f32[3,1,3,2048]{3,2,1,0:T(4,128)S(1)}, u32[]{:S(2)}, u32[]{:S(2)}) collective-permute-start(f32[3,1,3,2048]{3,2,1,0:T(4,128)S(1)} %get-tuple-element.25), channel_id=1, source_target_pairs={{4,0},{8,4},{12,8},{16,12},{20,16},{24,20},{28,24},{32,28},{36,32}... | collective-permute-start | bytes 221192 | tf_op jit(solution)/shard_map/ppermute | solution.py:26
  24.7 14.4 %collective-permute-start.2 = (f32[3,1,3,2048]{3,2,1,0:T(4,128)S(1)}, f32[3,1,3,2048]{3,2,1,0:T(4,128)S(1)}, u32[]{:S(2)}, u32[]{:S(2)}) collective-permute-start(f32[3,1,3,2048]{3,2,1,0:T(4,128)S(1)} %get-tuple-element.26), channel_id=1, source_target_pairs={{0,4},{4,8},{8,12},{12,16},{16,20},{20,24},{24,28},{28,32},{32,36}... | collective-permute-start | bytes 221192 | tf_op jit(solution)/shard_map/ppermute | solution.py:25
  27.3 21.2 %copy-start.7 = (f32[32,32]{1,0:T(8,128)}, f32[32,32]{1,0:T(8,128)S(1)}, u32[]{:S(2)}) copy-start(f32[32,32]{1,0:T(8,128)S(1)} %fusion.103) | copy-start | bytes 12292
  28.3 19.6 %copy-start.5 = (f32[32,32]{1,0:T(8,128)}, f32[32,32]{1,0:T(8,128)S(1)}, u32[]{:S(2)}) copy-start(f32[32,32]{1,0:T(8,128)S(1)} %fusion.102) | copy-start | bytes 12292
  39.2 2.2 %copy-start.9 = (f32[3]{0:T(128)S(1)}, f32[3]{0:T(128)}, u32[]{:S(2)}) copy-start(f32[3]{0:T(128)} %constant.97.clone) | copy-start | bytes 40
  51.5 2.1 %copy-start.4 = (f32[48,128,16]{1,2,0:T(8,128)S(1)}, f32[48,128,16]{1,2,0:T(8,128)}, u32[]{:S(2)}) copy-start(f32[48,128,16]{1,2,0:T(8,128)} %fusion.48) | copy-start | bytes 1179652
  56.2 26.3 %copy-start.10 = (f32[3]{0:T(128)S(1)}, f32[3]{0:T(128)}, u32[]{:S(2)}) copy-start(f32[3]{0:T(128)} %constant.97.clone) | copy-start | bytes 40
  56.2 25.1 %collective-permute-start.5 = (f32[3,1,16,2048]{3,2,1,0:T(8,128)S(1)}, f32[3,1,16,2048]{3,2,1,0:T(8,128)S(1)}, u32[]{:S(2)}, u32[]{:S(2)}) collective-permute-start(f32[3,1,16,2048]{3,2,1,0:T(8,128)S(1)} %fusion.35), channel_id=1, source_target_pairs={{0,256},{4,260},{8,264},{12,268},{16,272},{20,276},{24,280},{28,28... | collective-permute-start | bytes 1179656 | tf_op jit(solution)/shard_map/ppermute | solution.py:32
  63.9 5.2 %collective-permute-start.6 = (f32[3,1,3,2048]{3,2,1,0:T(4,128)S(1)}, f32[3,1,3,2048]{3,2,1,0:T(4,128)S(1)}, u32[]{:S(2)}, u32[]{:S(2)}) collective-permute-start(f32[3,1,3,2048]{3,2,1,0:T(4,128)S(1)} %get-tuple-element.19), channel_id=1, source_target_pairs={{4,0},{8,4},{12,8},{16,12},{20,16},{24,20},{28,24},{32,28},{36,32}... | collective-permute-start | bytes 221192 | tf_op jit(solution)/shard_map/ppermute | solution.py:26
  65.8 14.3 %collective-permute-start.7 = (f32[3,1,3,2048]{3,2,1,0:T(4,128)S(1)}, f32[3,1,3,2048]{3,2,1,0:T(4,128)S(1)}, u32[]{:S(2)}, u32[]{:S(2)}) collective-permute-start(f32[3,1,3,2048]{3,2,1,0:T(4,128)S(1)} %get-tuple-element.20), channel_id=1, source_target_pairs={{0,4},{4,8},{8,12},{12,16},{16,20},{20,24},{24,28},{28,32},{32,36}... | collective-permute-start | bytes 221192 | tf_op jit(solution)/shard_map/ppermute | solution.py:25
  86.1 1.4 %copy-start.8 = (f32[32,32]{1,0:T(8,128)S(1)}, f32[32,32]{1,0:T(8,128)}, u32[]{:S(2)}) copy-start(f32[32,32]{1,0:T(8,128)} %copy-done.7) | copy-start | bytes 12292
  86.1 2.8 %copy-start.6 = (f32[32,32]{1,0:T(8,128)S(1)}, f32[32,32]{1,0:T(8,128)}, u32[]{:S(2)}) copy-start(f32[32,32]{1,0:T(8,128)} %copy-done.5) | copy-start | bytes 12292
  91.0 9.7 %copy-start.3 = (f32[48,128,16]{1,2,0:T(8,128)S(1)}, f32[48,128,16]{1,2,0:T(8,128)}, u32[]{:S(2)}) copy-start(f32[48,128,16]{1,2,0:T(8,128)} %fusion.50) | copy-start | bytes 1179652
  92.1 6.2 %copy-start.2 = (f32[3,1,16,2048]{3,2,1,0:T(8,128)}, f32[3,1,16,2048]{3,2,1,0:T(8,128)S(1)}, u32[]{:S(2)}) copy-start(f32[3,1,16,2048]{3,2,1,0:T(8,128)S(1)} %fusion.37) | copy-start | bytes 1179652
  93.9 8.4 %collective-permute-start.8 = (f32[1,16,2048]{2,1,0:T(8,128)}, f32[1,16,2048]{2,1,0:T(8,128)}, u32[]{:S(2)}, u32[]{:S(2)}) collective-permute-start(f32[1,16,2048]{2,1,0:T(8,128)} %get-tuple-element.14), channel_id=1, source_target_pairs={{1,0},{2,1},{3,2},{5,4},{6,5},{7,6},{9,8},{10,9},{11,10},{13,12},{... | collective-permute-start | bytes 393224 | tf_op jit(solution)/shard_map/ppermute | solution.py:26
  98.2 7.2 %collective-permute-start.9 = (f32[1,16,2048]{2,1,0:T(8,128)}, f32[1,16,2048]{2,1,0:T(8,128)}, u32[]{:S(2)}, u32[]{:S(2)}) collective-permute-start(f32[1,16,2048]{2,1,0:T(8,128)} %get-tuple-element.14), channel_id=1, source_target_pairs={{0,1},{1,2},{2,3},{4,5},{5,6},{6,7},{8,9},{9,10},{10,11},{12,13},{... | collective-permute-start | bytes 393224 | tf_op jit(solution)/shard_map/ppermute | solution.py:25
where the time goes:
time: 110 us; the launch traced here: 109 us
  starting transfers between devices  42.7 us (39%)
  waiting for transfers between devices  24.9 us (23%)
  matrix products  16.6 us (15%)
  other arithmetic  15.2 us (14%)
  local copies, waits for them, and re-layouts  8.4 us (8%)
  between operations  1.15 us (1%)
    ppermute x4, waiting for transfers between devices, with_halo(): before = lax.ppermute(last, axis, up)  24.9 us
    ppermute x4, starting transfers between devices, with_halo(): after = lax.ppermute(initial, axis, down)  19.2 us
    ppermute x2, starting transfers between devices, from_partner(): lax.ppermute(value, axis, [(i, i ^ 1 << bit) for i in range(lax.axis_size...  14.7 us
    dot_general x12, matrix products, small_product(): jnp.einsum('kn,bnp->bkp', table, values, precision=highest, preferred_ele...  11 us
    ppermute x4, starting transfers between devices, with_halo(): before = lax.ppermute(last, axis, up)  8.88 us
    add x2, other arithmetic, body(): -advect[1] - secant * zonal_slope[0] + coriolis_term * northward  2.84 us
    dot_general x2, matrix products, circle_transform(): jnp.dot(weighted.reshape(batch_size * blocks, 2 * radix_size), inverse_ta...  2.8 us
    dot_general x2, matrix products, circle_transform(): jnp.dot(joined, forward_table, precision=highest, preferred_element_type=...  2.78 us
  transfers between devices with their start and end apart: 10, of which 3 were waited for; matrix products, arithmetic and copies ran while one was open for 21% of the time, Pallas kernels for 0%

commit v1 on v0

v1 whole, which is shorter than its diff:
```python
import functools
import math

import jax
import jax.numpy as jnp
import numpy as np
from jax import lax
from jax.experimental import pallas as pl
from jax.experimental.pallas import tpu as pltpu
from jax.sharding import PartitionSpec as P

STEPS = 2
MESH = pl.DeviceIdType.MESH

courant = 0.2
mixing = 0.25
coriolis = 0.5
cos_floor = 0.25

LANES = 128
ROWS = 8
f32 = jnp.float32
bf16 = jnp.bfloat16


def rotate(z, angle):
    re, im = z
    c, s = math.cos(angle), math.sin(angle)
    if abs(s) < 1e-12:
        return (re, im) if c > 0 else (-re, -im)
    if abs(c) < 1e-12:
        return (-im, re) if s > 0 else (im, -re)
    return re * c - im * s, re * s + im * c


def complex_sum(values, sign):
    count = len(values)
    if count == 1:
        return values
    half = count // 2
    plus = [(a[0] + b[0], a[1] + b[1]) for a, b in zip(values[:half], values[half:])]
    minus = [(a[0] - b[0], a[1] - b[1]) for a, b in zip(values[:half], values[half:])]
    minus = [rotate(z, sign * 2 * math.pi * n / count) for n, z in enumerate(minus)]
    even, odd = complex_sum(plus, sign), complex_sum(minus, sign)
    return [z for pair in zip(even, odd) for z in pair]


def odd_frequencies(values):
    count = len(values)
    if count == 1:
        return {1: (values[0], None)}
    half = count // 2
    joined = [rotate((values[n], -values[n + half]), -math.pi * n / count) for n in range(half)]
    out = {}
    for t, (re, im) in enumerate(complex_sum(joined, -1)):
        k = 4 * t + 1
        if k <= count:
            out[k] = (re, im)
        else:
            out[2 * count - k] = (re, -im)
    return out


def real_transform(values):
    count = len(values)
    if count == 1:
        return {0: (values[0], None)}
    half = count // 2
    even = real_transform([values[n] + values[n + half] for n in range(half)])
    out = {2 * k: z for k, z in even.items()}
    out.update(odd_frequencies([values[n] - values[n + half] for n in range(half)]))
    return out


def padded_transform(values):
    out = {2 * k: z for k, z in real_transform(values).items()}
    out.update(odd_frequencies(values))
    return out


def odd_inverse(terms, count):
    if count == 1:
        return [terms[1][0]]
    half = count // 2
    joined = []
    for t in range(half):
        k = 4 * t + 1
        if k <= count:
            joined.append(terms[k])
        else:
            re, im = terms[2 * count - k]
            joined.append((re, -im))
    turned = [rotate(z, math.pi * n / count) for n, z in enumerate(complex_sum(joined, 1))]
    return [z[0] for z in turned] + [-z[1] for z in turned]


def real_inverse(terms, count):
    if count == 1:
        return [terms[0][0]]
    half = count // 2
    even = real_inverse({k // 2: z for k, z in terms.items() if k % 2 == 0}, half)
    odd = odd_inverse({k: z for k, z in terms.items() if k % 2}, half)
    return [a + b for a, b in zip(even, odd)] + [a - b for a, b in zip(even, odd)]


def padded_inverse(terms, count):
    even = real_inverse({k // 2: z for k, z in terms.items() if k % 2 == 0}, count)
    odd = odd_inverse({k: z for k, z in terms.items() if k % 2}, count)
    return [a + b for a, b in zip(even, odd)]


def split(value):
    high = value.astype(bf16)
    return high, (value - high.astype(f32)).astype(bf16)


def np_split(table):
    table = jnp.asarray(table.astype(np.float32))
    high = table.astype(bf16)
    return high, (table - high.astype(f32)).astype(bf16)


def tables(lat_count, lon_count):
    length = 2 * lat_count
    blocks = lat_count // LANES
    ring = 2 * blocks
    kept = length // 3
    reach = kept // ring + 1
    lane = np.arange(LANES)
    shift = np.where(lane < 2 * reach, lane - reach, 0)
    valid = (lane < 2 * reach).astype(np.float64)
    psi = 2 * np.pi * (lane[:, None] + 0.5) * shift[None, :] / LANES
    cos, sin = np.cos(psi) * valid, np.sin(psi) * valid
    forward = np.block([[cos, sin], [sin, -cos]])
    inverse = np.block([[cos.T, sin.T], [sin.T, -cos.T]])
    small = np.arange(blocks + 1)
    phi = 2 * np.pi * small[:, None] * (lane[None, :] + 0.5) / length
    twist = np.concatenate([np.cos(phi), np.sin(phi)], 1)
    index = small[:, None] + ring * shift[None, :]
    weight = np.where((small == 0) | (small == blocks), 1.0, 2.0)[:, None] / length
    weight = weight * (np.abs(index) <= kept) * valid
    slope = weight * 2 * np.pi * index / length
    factor = np.concatenate([weight, weight, slope, -slope], 1)
    latitude = (np.arange(lat_count) + 0.5) * (np.pi / lat_count) - 0.5 * np.pi
    secant = 1.0 / np.maximum(np.cos(latitude), cos_floor)
    line = np.zeros((8, lat_count))
    line[0] = secant / 60.0
    line[1] = coriolis * np.sin(latitude)
    fields = 3
    own = np.zeros((fields * lon_count, fields * lon_count))
    outer = np.zeros((fields * lon_count, 2 * fields * ROWS))
    for f in range(fields):
        for row in range(lon_count):
            for offset, value in ((1, 45.0), (2, -9.0), (3, 1.0)):
                for sign in (1, -1):
                    at = row + sign * offset
                    if at < 0:
                        outer[f * lon_count + row, f * ROWS + at + ROWS] = sign * value
                    elif at >= lon_count:
                        outer[f * lon_count + row, (fields + f) * ROWS + at - lon_count] = sign * value
                    else:
                        own[f * lon_count + row, f * lon_count + at] = sign * value
    own = np.concatenate([own, own], 1)
    outer = np.concatenate([outer, outer], 1)
    return (
        *np_split(forward),
        *np_split(inverse),
        jnp.asarray(twist.astype(np.float32)),
        jnp.asarray(factor.astype(np.float32)),
        jnp.asarray(line.astype(np.float32)),
        jnp.asarray(own.astype(np.float32)).astype(bf16),
        jnp.asarray(outer.astype(np.float32)).astype(bf16),
    )


def kernel(
    sizes, thick_ref, wind_ref, fwd_hi, fwd_lo, inv_hi, inv_lo, twist_ref, factor_ref, line_ref, own_ref, outer_ref,
    out_h, out_w, state, opposite, halo, levels, spec_in, gain_own, turned, zonal, smooth, slope, load_sem,
    anti_send, anti_recv, halo_send, halo_recv, lev_send, lev_recv,
):
    lon_size, lev_size = sizes
    fields, lon_count, lat_count = state.shape[1:]
    blocks = lat_count // LANES
    groups = lon_count // ROWS
    lon, lev = lax.axis_index("lon"), lax.axis_index("lev")
    right = lax.rem(lon + 1, lon_size)
    left = lax.rem(lon + lon_size - 1, lon_size)
    partner = lax.rem(lon + lon_size // 2, lon_size)
    has_below, has_above = lev > 0, lev < lev_size - 1

    loads = [pltpu.make_async_copy(thick_ref.at[0], state.at[0, 0], load_sem.at[0])]
    loads += [pltpu.make_async_copy(wind_ref.at[f, 0], state.at[0, f + 1], load_sem.at[f + 1]) for f in range(2)]
    for copy in loads:
        copy.start()
    halo[...] = jnp.zeros_like(halo)

    @pl.when(jnp.logical_not(has_below))
    def _():
        for s in range(STEPS):
            levels[s, 0] = jnp.zeros_like(levels[s, 0])

    @pl.when(jnp.logical_not(has_above))
    def _():
        for s in range(STEPS):
            levels[s, 1] = jnp.zeros_like(levels[s, 1])

    barrier = pltpu.get_barrier_semaphore()
    for at in (left, right, partner):
        pl.semaphore_signal(barrier, inc=1, device_id={"lon": at}, device_id_type=MESH)

    @pl.when(has_below)
    def _():
        pl.semaphore_signal(barrier, inc=1, device_id={"lev": lev - 1}, device_id_type=MESH)

    @pl.when(has_above)
    def _():
        pl.semaphore_signal(barrier, inc=1, device_id={"lev": lev + 1}, device_id_type=MESH)

    pl.semaphore_wait(barrier, 3 + has_below.astype(jnp.int32) + has_above.astype(jnp.int32))

    def rows(g):
        return pl.ds(g * ROWS, ROWS)

    def source(s, f, at):
        if s == 0:
            return thick_ref.at[0, at] if f == 0 else wind_ref.at[f - 1, 0, at]
        return state.at[s, f, at]

    def anti_copy(s, g, f):
        return pltpu.make_async_remote_copy(
            src_ref=source(s, f, rows(g)), dst_ref=opposite.at[s, f, rows(g)],
            send_sem=anti_send.at[s, g, f], recv_sem=anti_recv.at[s, g, f],
            device_id={"lon": partner}, device_id_type=MESH,
        )

    def halo_copy(s, side, f):
        start = lon_count - 3 if side == 0 else 0
        landing = ROWS - 3 if side == 0 else 0
        return pltpu.make_async_remote_copy(
            src_ref=source(s, f, pl.ds(start, 3)), dst_ref=halo.at[s, side, f, pl.ds(landing, 3)],
            send_sem=halo_send.at[s, side, f], recv_sem=halo_recv.at[s, side, f],
            device_id={"lon": right if side == 0 else left}, device_id_type=MESH,
        )

    def lev_copy(s, g, side):
        return pltpu.make_async_remote_copy(
            src_ref=source(s, 0, rows(g)), dst_ref=levels.at[s, side, rows(g)],
            send_sem=lev_send.at[s, g, side], recv_sem=lev_recv.at[s, g, side],
            device_id={"lev": lev + 1 if side == 0 else lev - 1}, device_id_type=MESH,
        )

    def send_halo(s, side):
        for f in range(fields):
            halo_copy(s, side, f).start()

    def send_group(s, g):
        for f in range(fields):
            anti_copy(s, g, f).start()

        @pl.when(has_above)
        def _():
            lev_copy(s, g, 0).start()

        @pl.when(has_below)
        def _():
            lev_copy(s, g, 1).start()

    def transform_half(ref, s, g):
        for f in range(fields):
            values = [ref[s, f, g * ROWS : (g + 1) * ROWS, n * LANES : (n + 1) * LANES] for n in range(blocks)]
            for k, (re, im) in padded_transform(values).items():
                at = (k * fields + f) * ROWS
                c, d = twist_ref[k : k + 1, :LANES], twist_ref[k : k + 1, LANES:]
                if k == 0:
                    out = (re, jnp.zeros_like(re))
                elif im is None:
                    out = (re * c, -re * d)
                else:
                    out = (re * c + im * d, im * c - re * d)
                spec_in[at : at + ROWS, :LANES] = out[0]
                spec_in[at : at + ROWS, LANES:] = out[1]
        return product(spec_in[...], fwd_hi, fwd_lo)

    def product(value, high, low):
        top, rest = split(value)
        out = jnp.dot(top, low[...], preferred_element_type=f32)
        out += jnp.dot(rest, high[...], preferred_element_type=f32)
        return out + jnp.dot(top, high[...], preferred_element_type=f32)

    def own_group(s, g):
        gain_own[g] = transform_half(state, s, g)

    def own_zonal(s):
        value = state[s].reshape(fields * lon_count, lat_count)
        zonal[...] = jnp.dot(own_ref[...], jnp.concatenate(split(value), 0), preferred_element_type=f32)

    def outer_zonal(s):
        for side in range(2):
            for f in range(fields):
                halo_copy(s, side, f).wait_recv()
        value = halo[s].reshape(2 * fields * ROWS, lat_count)
        zonal[...] += jnp.dot(outer_ref[...], jnp.concatenate(split(value), 0), preferred_element_type=f32)

    def back(g, which):
        target = smooth if which == 0 else slope
        for f in range(fields):
            terms = {}
            for k in range(blocks + 1):
                at = (k * fields + f) * ROWS
                re, im = turned[which, at : at + ROWS, :LANES], turned[which, at : at + ROWS, LANES:]
                c, d = twist_ref[k : k + 1, :LANES], twist_ref[k : k + 1, LANES:]
                if k == 0:
                    terms[k] = (re, None)
                elif k == blocks:
                    terms[k] = (re * c - im * d, None)
                else:
                    terms[k] = (re * c - im * d, re * d + im * c)
            for n, value in enumerate(padded_inverse(terms, blocks)):
                target[f, :, n * LANES : (n + 1) * LANES] = value

    def group(s, g):
        for f in range(fields):
            anti_copy(s, g, f).wait_recv()
        theirs = transform_half(opposite, s, g)
        mine = gain_own[g]
        first, second = [], []
        for k in range(blocks + 1):
            for f in range(fields):
                at = (k * fields + f) * ROWS
                sign = 1.0 if f == 0 else -1.0
                a = mine[at : at + ROWS, :LANES] + sign * theirs[at : at + ROWS, :LANES]
                b = mine[at : at + ROWS, LANES:] - sign * theirs[at : at + ROWS, LANES:]
                w = factor_ref[k : k + 1]
                turned[0, at : at + ROWS, :LANES] = a * w[:, :LANES]
                turned[0, at : at + ROWS, LANES:] = b * w[:, LANES : 2 * LANES]
                turned[1, at : at + ROWS, :LANES] = b * w[:, 2 * LANES : 3 * LANES]
                turned[1, at : at + ROWS, LANES:] = a * w[:, 3 * LANES :]
        for which in range(2):
            turned[which] = product(turned[which], inv_hi, inv_lo)
        for which in range(2):
            back(g, which)

        @pl.when(has_below)
        def _():
            lev_copy(s, g, 0).wait_recv()

        @pl.when(has_above)
        def _():
            lev_copy(s, g, 1).wait_recv()

        r = slice(g * ROWS, (g + 1) * ROWS)
        for n in range(blocks):
            lanes = slice(n * LANES, (n + 1) * LANES)
            h, u, v = (state[s, f, r, lanes] for f in range(fields))
            secant, turn = line_ref[0:1, lanes], line_ref[1:2, lanes]
            zh, zu, zv = (
                zonal[f * lon_count + g * ROWS : f * lon_count + (g + 1) * ROWS, lanes] * secant for f in range(fields)
            )
            mh, mu, mv = (slope[f, :, lanes] for f in range(fields))
            vertical = levels[s, 0, r, lanes] + levels[s, 1, r, lanes] - 2.0 * h
            th = mixing * vertical - (u * zh + v * mh) - h * (zu + mv)
            tu = turn * v - (u * zu + v * mu) - zh
            tv = -(u * zv + v * mv) - mh - turn * u
            nh, nu, nv = (smooth[f, :, lanes] + courant * t for f, t in enumerate((th, tu, tv)))
            if s < STEPS - 1:
                state[s + 1, 0, r, lanes] = nh
                state[s + 1, 1, r, lanes] = nu
                state[s + 1, 2, r, lanes] = nv
            else:
                out_h[0, r, lanes] = nh
                out_w[0, 0, r, lanes] = nu
                out_w[1, 0, r, lanes] = nv

    send_halo(0, 0)
    send_halo(0, 1)
    for g in range(groups):
        send_group(0, g)
    for copy in loads:
        copy.wait()
    for s in range(STEPS):
        if s == 0:
            own_group(s, 0)
        own_group(s, groups - 1)
        own_zonal(s)
        outer_zonal(s)
        for g in range(groups):
            group(s, g)
            if s < STEPS - 1:
                send_group(s + 1, g)
                if g == 0:
                    send_halo(s + 1, 1)
                    own_group(s + 1, 0)
                else:
                    send_halo(s + 1, 0)
    for s in range(STEPS):
        for g in range(groups):
            for f in range(fields):
                anti_copy(s, g, f).wait_send()

            @pl.when(has_above)
            def _():
                lev_copy(s, g, 0).wait_send()

            @pl.when(has_below)
            def _():
                lev_copy(s, g, 1).wait_send()

        for side in range(2):
            for f in range(fields):
                halo_copy(s, side, f).wait_send()


def body(sizes, thickness, wind_field):
    level_count, lon_count, lat_count = thickness.shape
    fields = 3
    groups = lon_count // ROWS
    blocks = lat_count // LANES
    spectral_rows = (blocks + 1) * fields * ROWS
    consts = tables(lat_count, lon_count)
    vmem = pl.BlockSpec(memory_space=pltpu.VMEM)
    hbm = pl.BlockSpec(memory_space=pl.ANY)
    dma = pltpu.SemaphoreType.DMA
    return pl.pallas_call(
        functools.partial(kernel, sizes),
        out_shape=(
            jax.ShapeDtypeStruct(thickness.shape, f32),
            jax.ShapeDtypeStruct(wind_field.shape, f32),
        ),
        in_specs=[hbm, hbm] + [vmem] * len(consts),
        out_specs=(vmem, vmem),
        scratch_shapes=[
            pltpu.VMEM((STEPS, fields, lon_count, lat_count), f32),
            pltpu.VMEM((STEPS, fields, lon_count, lat_count), f32),
            pltpu.VMEM((STEPS, 2, fields, ROWS, lat_count), f32),
            pltpu.VMEM((STEPS, 2, lon_count, lat_count), f32),
            pltpu.VMEM((spectral_rows, 2 * LANES), f32),
            pltpu.VMEM((groups, spectral_rows, 2 * LANES), f32),
            pltpu.VMEM((2, spectral_rows, 2 * LANES), f32),
            pltpu.VMEM((fields * lon_count, lat_count), f32),
            pltpu.VMEM((fields, ROWS, lat_count), f32),
            pltpu.VMEM((fields, ROWS, lat_count), f32),
            dma((fields,)),
            dma((STEPS, groups, fields)),
            dma((STEPS, groups, fields)),
            dma((STEPS, 2, fields)),
            dma((STEPS, 2, fields)),
            dma((STEPS, groups, 2)),
            dma((STEPS, groups, 2)),
        ],
        name="sphere_steps",
        compiler_params=pltpu.CompilerParams(collective_id=0, has_side_effects=True, vmem_limit_bytes=40 << 20),
    )(thickness, wind_field, *consts)


def solution(mesh):
    sizes = (mesh.shape["lon"], mesh.shape["lev"])
    in_specs = (P("lev", "lon", None), P(None, "lev", "lon", None))
    out_specs = (P("lev", "lon", None), P(None, "lev", "lon", None))
    return jax.shard_map(
        functools.partial(body, sizes), mesh=mesh, in_specs=in_specs, out_specs=out_specs, check_vma=False
    )
```

time: 110 us -> 67.9 us (0.62)
  the two profiles are of different devices: /device:TPU:64 before, /device:TPU:6 now
where the time goes in v1:
time: 67.9 us; the launch traced here: 67.4 us
  Pallas kernels  56.1 us (83%)
  local copies, waits for them, and re-layouts  10.6 us (16%)
    pallas_call x1, Pallas kernels, body(): pl.pallas_call(functools.partial(kernel, sizes), out_shape=(jax.ShapeDtyp...  56.1 us
    unnamed x24, local copies, waits for them, and re-layouts  10.6 us

profile of v1, /device:TPU:6, one launch (start us, length us, event | category | flops | bytes accessed | tf_op | source)
XLA Modules:
  0.0 67.4 jit_solution(5137259278833815092)
XLA Ops:
  0.6 0.0 copy-start.9
  0.6 0.7 %copy-done.9 = bf16[48,96]{1,0:T(8,128)(2,1)S(1)} copy-done((bf16[48,96]{1,0:T(8,128)(2,1)S(1)}, bf16[48,96]{1,0:T(8,128)(2,1)}, u32[]{:S(2)}) %copy-start.9) | copy-done | bytes 9240
  1.3 0.0 copy-start
  1.3 0.9 %copy-done = f32[2,1,16,2048]{3,2,1,0:T(8,128)S(1)} copy-done((f32[2,1,16,2048]{3,2,1,0:T(8,128)S(1)}, f32[2,1,16,2048]{3,2,1,0:T(8,128)}, u32[]{:S(2)}) %copy-start) | copy-done | bytes 262168
  2.3 0.0 copy-start.1
  2.3 0.9 %copy-done.1 = f32[1,16,2048]{2,1,0:T(8,128)S(1)} copy-done((f32[1,16,2048]{2,1,0:T(8,128)S(1)}, f32[1,16,2048]{2,1,0:T(8,128)}, u32[]{:S(2)}) %copy-start.1) | copy-done | bytes 131096
  3.2 0.0 copy-start.2
  3.2 0.9 %copy-done.2 = bf16[256,256]{1,0:T(8,128)(2,1)S(1)} copy-done((bf16[256,256]{1,0:T(8,128)(2,1)S(1)}, bf16[256,256]{1,0:T(8,128)(2,1)}, u32[]{:S(2)}) %copy-start.2) | copy-done | bytes 131096
  4.1 0.0 copy-start.3
  4.1 0.9 %copy-done.3 = bf16[256,256]{1,0:T(8,128)(2,1)S(1)} copy-done((bf16[256,256]{1,0:T(8,128)(2,1)S(1)}, bf16[256,256]{1,0:T(8,128)(2,1)}, u32[]{:S(2)}) %copy-start.3) | copy-done | bytes 131096
  5.0 0.0 copy-start.4
  5.0 0.9 %copy-done.4 = bf16[256,256]{1,0:T(8,128)(2,1)S(1)} copy-done((bf16[256,256]{1,0:T(8,128)(2,1)S(1)}, bf16[256,256]{1,0:T(8,128)(2,1)}, u32[]{:S(2)}) %copy-start.4) | copy-done | bytes 131096
  5.9 0.0 copy-start.5
  5.9 0.9 %copy-done.5 = bf16[256,256]{1,0:T(8,128)(2,1)S(1)} copy-done((bf16[256,256]{1,0:T(8,128)(2,1)S(1)}, bf16[256,256]{1,0:T(8,128)(2,1)}, u32[]{:S(2)}) %copy-start.5) | copy-done | bytes 131096
  6.8 0.0 copy-start.6
  6.8 0.8 %copy-done.6 = f32[8,2048]{1,0:T(8,128)S(1)} copy-done((f32[8,2048]{1,0:T(8,128)S(1)}, f32[8,2048]{1,0:T(8,128)}, u32[]{:S(2)}) %copy-start.6) | copy-done | bytes 65560
  7.7 0.0 copy-start.7
  7.7 0.8 %copy-done.7 = f32[17,512]{1,0:T(8,128)S(1)} copy-done((f32[17,512]{1,0:T(8,128)S(1)}, f32[17,512]{1,0:T(8,128)}, u32[]{:S(2)}) %copy-start.7) | copy-done | bytes 34840
  8.5 0.0 copy-start.8
  8.5 0.7 %copy-done.8 = f32[17,256]{1,0:T(8,128)S(1)} copy-done((f32[17,256]{1,0:T(8,128)S(1)}, f32[17,256]{1,0:T(8,128)}, u32[]{:S(2)}) %copy-start.8) | copy-done | bytes 17432
  9.2 0.0 copy-start.10
  9.2 0.7 %copy-done.10 = bf16[48,96]{1,0:T(8,128)(2,1)S(1)} copy-done((bf16[48,96]{1,0:T(8,128)(2,1)S(1)}, bf16[48,96]{1,0:T(8,128)(2,1)}, u32[]{:S(2)}) %copy-start.10) | copy-done | bytes 9240
  9.9 56.1 %sphere_steps.1 = (f32[1,16,2048]{2,1,0:T(8,128)S(1)}, f32[2,1,16,2048]{3,2,1,0:T(8,128)S(1)}) custom-call(f32[1,16,2048]{2,1,0:T(8,128)S(1)} %copy-done.1, f32[2,1,16,2048]{3,2,1,0:T(8,128)S(1)} %copy-done, bf16[256,256]{1,0:T(8,128)(2,1)S(1)} %copy-done.5, bf16[256,256]{1,0:T(8,128)(2,1)S(1)} %copy-done.4, bf16[256,256]{1,0:T(8,128)(2,1)S(1)} %copy-done.3, ...), custom_call_target="tpu_custom_call" | custom-call | tf_op jit(solution)/shard_map/sphere_steps/pallas_call | solution.py:423
  66.0 0.7 copy.13
  66.7 0.7 %copy.14 = f32[2,1,16,2048]{3,2,1,0:T(8,128)} copy(f32[2,1,16,2048]{3,2,1,0:T(8,128)S(1)} %get-tuple-element.5) | data formatting | bytes 524288
Async XLA Ops:
  0.6 0.7 %copy-start.9 = (bf16[48,96]{1,0:T(8,128)(2,1)S(1)}, bf16[48,96]{1,0:T(8,128)(2,1)}, u32[]{:S(2)}) copy-start(bf16[48,96]{1,0:T(8,128)(2,1)} %constant.32.outer_ref) | copy-start | bytes 27652
  1.3 0.9 %copy-start = (f32[2,1,16,2048]{3,2,1,0:T(8,128)S(1)}, f32[2,1,16,2048]{3,2,1,0:T(8,128)}, u32[]{:S(2)}) copy-start(f32[2,1,16,2048]{3,2,1,0:T(8,128)} %wind_ref.1) | copy-start | bytes 786436
  2.3 0.9 %copy-start.1 = (f32[1,16,2048]{2,1,0:T(8,128)S(1)}, f32[1,16,2048]{2,1,0:T(8,128)}, u32[]{:S(2)}) copy-start(f32[1,16,2048]{2,1,0:T(8,128)} %thick_ref.1) | copy-start | bytes 393220
  3.2 0.9 %copy-start.2 = (bf16[256,256]{1,0:T(8,128)(2,1)S(1)}, bf16[256,256]{1,0:T(8,128)(2,1)}, u32[]{:S(2)}) copy-start(bf16[256,256]{1,0:T(8,128)(2,1)} %constant.30.inv_lo) | copy-start | bytes 393220
  4.1 0.9 %copy-start.3 = (bf16[256,256]{1,0:T(8,128)(2,1)S(1)}, bf16[256,256]{1,0:T(8,128)(2,1)}, u32[]{:S(2)}) copy-start(bf16[256,256]{1,0:T(8,128)(2,1)} %constant.27.inv_hi) | copy-start | bytes 393220
  5.0 0.9 %copy-start.4 = (bf16[256,256]{1,0:T(8,128)(2,1)S(1)}, bf16[256,256]{1,0:T(8,128)(2,1)}, u32[]{:S(2)}) copy-start(bf16[256,256]{1,0:T(8,128)(2,1)} %constant.26.fwd_lo) | copy-start | bytes 393220
  5.9 0.9 %copy-start.5 = (bf16[256,256]{1,0:T(8,128)(2,1)S(1)}, bf16[256,256]{1,0:T(8,128)(2,1)}, u32[]{:S(2)}) copy-start(bf16[256,256]{1,0:T(8,128)(2,1)} %constant.23.fwd_hi) | copy-start | bytes 393220
  6.8 0.8 %copy-start.6 = (f32[8,2048]{1,0:T(8,128)S(1)}, f32[8,2048]{1,0:T(8,128)}, u32[]{:S(2)}) copy-start(f32[8,2048]{1,0:T(8,128)} %constant.18.clone.line_ref) | copy-start | bytes 196612
  7.7 0.8 %copy-start.7 = (f32[17,512]{1,0:T(8,128)S(1)}, f32[17,512]{1,0:T(8,128)}, u32[]{:S(2)}) copy-start(f32[17,512]{1,0:T(8,128)} %constant.17.clone.factor_ref) | copy-start | bytes 104452
  8.5 0.7 %copy-start.8 = (f32[17,256]{1,0:T(8,128)S(1)}, f32[17,256]{1,0:T(8,128)}, u32[]{:S(2)}) copy-start(f32[17,256]{1,0:T(8,128)} %constant.16.clone.twist_ref) | copy-start | bytes 52228
  9.2 0.7 %copy-start.10 = (bf16[48,96]{1,0:T(8,128)(2,1)S(1)}, bf16[48,96]{1,0:T(8,128)(2,1)}, u32[]{:S(2)}) copy-start(bf16[48,96]{1,0:T(8,128)(2,1)} %constant.31.own_ref) | copy-start | bytes 27652

commit v2 on v1

--- a/solution.py
+++ b/solution.py
@@ -174,24 +174,35 @@
 
 
 def kernel(
-    sizes, thick_ref, wind_ref, fwd_hi, fwd_lo, inv_hi, inv_lo, twist_ref, factor_ref, line_ref, own_ref, outer_ref,
-    out_h, out_w, state, opposite, halo, levels, spec_in, gain_own, turned, zonal, smooth, slope, load_sem,
-    anti_send, anti_recv, halo_send, halo_recv, lev_send, lev_recv,
+    sizes, const_shapes, thick_ref, wind_ref, *refs,
 ):
+    count = len(const_shapes)
+    const_hbm, (out_h, out_w), scratch = refs[:count], refs[count : count + 2], refs[count + 2 :]
+    const_refs, scratch = scratch[:count], scratch[count:]
+    fwd_hi, fwd_lo, inv_hi, inv_lo, twist_ref, factor_ref, line_ref, own_ref, outer_ref = const_refs
+    (
+        state, opposite, halo, levels, spec_in, gain_own, turned, zonal, smooth, slope, load_sem, const_sem,
+        anti_send, anti_recv, halo_send, halo_recv, lev_send, lev_recv,
+    ) = scratch
     lon_size, lev_size = sizes
     fields, lon_count, lat_count = state.shape[1:]
     blocks = lat_count // LANES
     groups = lon_count // ROWS
+    half = lon_size // 2
     lon, lev = lax.axis_index("lon"), lax.axis_index("lev")
-    right = lax.rem(lon + 1, lon_size)
-    left = lax.rem(lon + lon_size - 1, lon_size)
-    partner = lax.rem(lon + lon_size // 2, lon_size)
+    place = lax.rem(lon, half)
+    base = lon - place
+    right = base + lax.rem(place + 1, half)
+    left = base + lax.rem(place + half - 1, half)
+    partner = lax.rem(lon + half, lon_size)
+    at_end, at_start = place == half - 1, place == 0
+    not_end, not_start = place < half - 1, place > 0
+    flip = at_end.astype(jnp.int32)
     has_below, has_above = lev > 0, lev < lev_size - 1
 
     loads = [pltpu.make_async_copy(thick_ref.at[0], state.at[0, 0], load_sem.at[0])]
     loads += [pltpu.make_async_copy(wind_ref.at[f, 0], state.at[0, f + 1], load_sem.at[f + 1]) for f in range(2)]
-    for copy in loads:
-        copy.start()
+    loads += [pltpu.make_async_copy(const_hbm[n], const_refs[n], const_sem.at[n]) for n in range(count)]
     halo[...] = jnp.zeros_like(halo)
 
     @pl.when(jnp.logical_not(has_below))
@@ -205,7 +216,7 @@
             levels[s, 1] = jnp.zeros_like(levels[s, 1])
 
     barrier = pltpu.get_barrier_semaphore()
-    for at in (left, right, partner):
+    for at in (partner, left, right):
         pl.semaphore_signal(barrier, inc=1, device_id={"lon": at}, device_id_type=MESH)
 
     @pl.when(has_below)
@@ -216,10 +227,13 @@
     def _():
         pl.semaphore_signal(barrier, inc=1, device_id={"lev": lev + 1}, device_id_type=MESH)
 
+    for copy in loads:
+        copy.start()
     pl.semaphore_wait(barrier, 3 + has_below.astype(jnp.int32) + has_above.astype(jnp.int32))
 
     def rows(g):
-        return pl.ds(g * ROWS, ROWS)
+        index = g + flip * (groups - 1 - 2 * g)
+        return pl.ds(pl.multiple_of(index * ROWS, ROWS), ROWS)
 
     def source(s, f, at):
         if s == 0:
@@ -233,11 +247,12 @@
             device_id={"lon": partner}, device_id_type=MESH,
         )
 
-    def halo_copy(s, side, f):
-        start = lon_count - 3 if side == 0 else 0
+    def halo_copy(s, side, f, relay=False):
+        at = pl.ds(lon_count - 3 if side == 0 else 0, 3)
         landing = ROWS - 3 if side == 0 else 0
         return pltpu.make_async_remote_copy(
-            src_ref=source(s, f, pl.ds(start, 3)), dst_ref=halo.at[s, side, f, pl.ds(landing, 3)],
+            src_ref=opposite.at[s, f, at] if relay else source(s, f, at),
+            dst_ref=halo.at[s, side, f, pl.ds(landing, 3)],
             send_sem=halo_send.at[s, side, f], recv_sem=halo_recv.at[s, side, f],
             device_id={"lon": right if side == 0 else left}, device_id_type=MESH,
         )
@@ -249,9 +264,21 @@
             device_id={"lev": lev + 1 if side == 0 else lev - 1}, device_id_type=MESH,
         )
 
-    def send_halo(s, side):
-        for f in range(fields):
-            halo_copy(s, side, f).start()
+    def send_halo(s):
+        for side, inner in ((0, not_end), (1, not_start)):
+
+            @pl.when(inner)
+            def _(side=side):
+                for f in range(fields):
+                    halo_copy(s, side, f).start()
+
+    def relay_halo(s):
+        for side, outer in ((0, at_end), (1, at_start)):
+
+            @pl.when(outer)
+            def _(side=side):
+                for f in range(fields):
+                    halo_copy(s, side, f, True).start()
 
     def send_group(s, g):
         for f in range(fields):
@@ -264,22 +291,6 @@
         @pl.when(has_below)
         def _():
             lev_copy(s, g, 1).start()
-
-    def transform_half(ref, s, g):
-        for f in range(fields):
-            values = [ref[s, f, g * ROWS : (g + 1) * ROWS, n * LANES : (n + 1) * LANES] for n in range(blocks)]
-            for k, (re, im) in padded_transform(values).items():
-                at = (k * fields + f) * ROWS
-                c, d = twist_ref[k : k + 1, :LANES], twist_ref[k : k + 1, LANES:]
-                if k == 0:
-                    out = (re, jnp.zeros_like(re))
-                elif im is None:
-                    out = (re * c, -re * d)
-                else:
-                    out = (re * c + im * d, im * c - re * d)
-                spec_in[at : at + ROWS, :LANES] = out[0]
-                spec_in[at : at + ROWS, LANES:] = out[1]
-        return product(spec_in[...], fwd_hi, fwd_lo)
 
     def product(value, high, low):
         top, rest = split(value)
@@ -287,8 +298,24 @@
         out += jnp.dot(rest, high[...], preferred_element_type=f32)
         return out + jnp.dot(top, high[...], preferred_element_type=f32)
 
+    def transform_half(ref, s, g, f):
+        values = [ref[s, f, rows(g), n * LANES : (n + 1) * LANES] for n in range(blocks)]
+        for k, (re, im) in padded_transform(values).items():
+            at = k * ROWS
+            c, d = twist_ref[k : k + 1, :LANES], twist_ref[k : k + 1, LANES:]
+            if k == 0:
+                out = (re, jnp.zeros_like(re))
+            elif im is None:
+                out = (re * c, -re * d)
+            else:
+                out = (re * c + im * d, im * c - re * d)
+            spec_in[at : at + ROWS, :LANES] = out[0]
+            spec_in[at : at + ROWS, LANES:] = out[1]
+        return product(spec_in[...], fwd_hi, fwd_lo)
+
     def own_group(s, g):
-        gain_own[g] = transform_half(state, s, g)
+        for f in range(fields):
+            gain_own[g, f] = transform_half(state, s, g, f)
 
     def own_zonal(s):
         value = state[s].reshape(fields * lon_count, lat_count)
@@ -301,44 +328,47 @@
         value = halo[s].reshape(2 * fields * ROWS, lat_count)
         zonal[...] += jnp.dot(outer_ref[...], jnp.concatenate(split(value), 0), preferred_element_type=f32)
 
-    def back(g, which):
+    spectral = (blocks + 1) * ROWS
+
+    def back(f, which):
         target = smooth if which == 0 else slope
-        for f in range(fields):
-            terms = {}
-            for k in range(blocks + 1):
-                at = (k * fields + f) * ROWS
-                re, im = turned[which, at : at + ROWS, :LANES], turned[which, at : at + ROWS, LANES:]
-                c, d = twist_ref[k : k + 1, :LANES], twist_ref[k : k + 1, LANES:]
-                if k == 0:
-                    terms[k] = (re, None)
-                elif k == blocks:
-                    terms[k] = (re * c - im * d, None)
-                else:
-                    terms[k] = (re * c - im * d, re * d + im * c)
-            for n, value in enumerate(padded_inverse(terms, blocks)):
-                target[f, :, n * LANES : (n + 1) * LANES] = value
+        terms = {}
+        for k in range(blocks + 1):
+            at = which * spectral + k * ROWS
+            re, im = turned[at : at + ROWS, :LANES], turned[at : at + ROWS, LANES:]
+            c, d = twist_ref[k : k + 1, :LANES], twist_ref[k : k + 1, LANES:]
+            if k == 0:
+                terms[k] = (re, None)
+            elif k == blocks:
+                terms[k] = (re * c - im * d, None)
+            else:
+                terms[k] = (re * c - im * d, re * d + im * c)
+        for n, value in enumerate(padded_inverse(terms, blocks)):
+            target[f, :, n * LANES : (n + 1) * LANES] = value
 
     def group(s, g):
         for f in range(fields):
             anti_copy(s, g, f).wait_recv()
-        theirs = transform_half(opposite, s, g)
-        mine = gain_own[g]
-        first, second = [], []
-        for k in range(blocks + 1):
-            for f in range(fields):
-                at = (k * fields + f) * ROWS
-                sign = 1.0 if f == 0 else -1.0
+            if g == 0 and f == fields - 1:
+                relay_halo(s)
+            theirs = transform_half(opposite, s, g, f)
+            mine = gain_own[g, f]
+            sign = 1.0 if f == 0 else -1.0
+            for k in range(blocks + 1):
+                at = k * ROWS
                 a = mine[at : at + ROWS, :LANES] + sign * theirs[at : at + ROWS, :LANES]
                 b = mine[at : at + ROWS, LANES:] - sign * theirs[at : at + ROWS, LANES:]
                 w = factor_ref[k : k + 1]
-                turned[0, at : at + ROWS, :LANES] = a * w[:, :LANES]
-                turned[0, at : at + ROWS, LANES:] = b * w[:, LANES : 2 * LANES]
-                turned[1, at : at + ROWS, :LANES] = b * w[:, 2 * LANES : 3 * LANES]
-                turned[1, at : at + ROWS, LANES:] = a * w[:, 3 * LANES :]
-        for which in range(2):
-            turned[which] = product(turned[which], inv_hi, inv_lo)
-        for which in range(2):
-            back(g, which)
+                turned[at : at + ROWS, :LANES] = a * w[:, :LANES]
+                turned[at : at + ROWS, LANES:] = b * w[:, LANES : 2 * LANES]
+                at += spectral
+                turned[at : at + ROWS, :LANES] = b * w[:, 2 * LANES : 3 * LANES]
+                turned[at : at + ROWS, LANES:] = a * w[:, 3 * LANES :]
+            turned[...] = product(turned[...], inv_hi, inv_lo)
+            for which in range(2):
+                back(f, which)
+        if g == 0:
+            outer_zonal(s)
 
         @pl.when(has_below)
         def _():
@@ -348,14 +378,12 @@
         def _():
             lev_copy(s, g, 1).wait_recv()
 
-        r = slice(g * ROWS, (g + 1) * ROWS)
+        r = rows(g)
         for n in range(blocks):
             lanes = slice(n * LANES, (n + 1) * LANES)
             h, u, v = (state[s, f, r, lanes] for f in range(fields))
             secant, turn = line_ref[0:1, lanes], line_ref[1:2, lanes]
-            zh, zu, zv = (
-                zonal[f * lon_count + g * ROWS : f * lon_count + (g + 1) * ROWS, lanes] * secant for f in range(fields)
-            )
+            zh, zu, zv = (zonal[pl.ds(f * lon_count + r.start, ROWS), lanes] * secant for f in range(fields))
             mh, mu, mv = (slope[f, :, lanes] for f in range(fields))
             vertical = levels[s, 0, r, lanes] + levels[s, 1, r, lanes] - 2.0 * h
             th = mixing * vertical - (u * zh + v * mh) - h * (zu + mv)
@@ -371,27 +399,23 @@
                 out_w[0, 0, r, lanes] = nu
                 out_w[1, 0, r, lanes] = nv
 
-    send_halo(0, 0)
-    send_halo(0, 1)
     for g in range(groups):
         send_group(0, g)
+        if g == 0:
+            send_halo(0)
     for copy in loads:
         copy.wait()
+    for g in range(groups):
+        own_group(0, g)
     for s in range(STEPS):
-        if s == 0:
-            own_group(s, 0)
-        own_group(s, groups - 1)
         own_zonal(s)
-        outer_zonal(s)
         for g in range(groups):
             group(s, g)
             if s < STEPS - 1:
                 send_group(s + 1, g)
-                if g == 0:
-                    send_halo(s + 1, 1)
-                    own_group(s + 1, 0)
-                else:
-                    send_halo(s + 1, 0)
+                if g == groups - 1:
+                    send_halo(s + 1)
+                own_group(s + 1, g)
     for s in range(STEPS):
         for g in range(groups):
             for f in range(fields):
@@ -415,31 +439,33 @@
     fields = 3
     groups = lon_count // ROWS
     blocks = lat_count // LANES
-    spectral_rows = (blocks + 1) * fields * ROWS
+    spectral = (blocks + 1) * ROWS
     consts = tables(lat_count, lon_count)
     vmem = pl.BlockSpec(memory_space=pltpu.VMEM)
-    hbm = pl.BlockSpec(memory_space=pl.ANY)
+    hbm = pl.BlockSpec(memory_space=pltpu.HBM)
     dma = pltpu.SemaphoreType.DMA
     return pl.pallas_call(
-        functools.partial(kernel, sizes),
+        functools.partial(kernel, sizes, [c.shape for c in consts]),
         out_shape=(
             jax.ShapeDtypeStruct(thickness.shape, f32),
             jax.ShapeDtypeStruct(wind_field.shape, f32),
         ),
-        in_specs=[hbm, hbm] + [vmem] * len(consts),
+        in_specs=[hbm, hbm] + [hbm] * len(consts),
         out_specs=(vmem, vmem),
-        scratch_shapes=[
+        scratch_shapes=[pltpu.VMEM(c.shape, c.dtype) for c in consts]
+        + [
             pltpu.VMEM((STEPS, fields, lon_count, lat_count), f32),
             pltpu.VMEM((STEPS, fields, lon_count, lat_count), f32),
             pltpu.VMEM((STEPS, 2, fields, ROWS, lat_count), f32),
             pltpu.VMEM((STEPS, 2, lon_count, lat_count), f32),
-            pltpu.VMEM((spectral_rows, 2 * LANES), f32),
-            pltpu.VMEM((groups, spectral_rows, 2 * LANES), f32),
-            pltpu.VMEM((2, spectral_rows, 2 * LANES), f32),
+            pltpu.VMEM((spectral, 2 * LANES), f32),
+            pltpu.VMEM((groups, fields, spectral, 2 * LANES), f32),
+            pltpu.VMEM((2 * spectral, 2 * LANES), f32),
             pltpu.VMEM((fields * lon_count, lat_count), f32),
             pltpu.VMEM((fields, ROWS, lat_count), f32),
             pltpu.VMEM((fields, ROWS, lat_count), f32),
             dma((fields,)),
+            dma((len(consts),)),
             dma((STEPS, groups, fields)),
             dma((STEPS, groups, fields)),
             dma((STEPS, 2, fields)),
@@ -448,7 +474,7 @@
             dma((STEPS, groups, 2)),
         ],
         name="sphere_steps",
-        compiler_params=pltpu.CompilerParams(collective_id=0, has_side_effects=True, vmem_limit_bytes=40 << 20),
+        compiler_params=pltpu.CompilerParams(collective_id=0, has_side_effects=True, vmem_limit_bytes=67_043_328),
     )(thickness, wind_field, *consts)
 
 

time: 67.9 us -> 55.8 us (0.82)
  the two profiles are of different devices: /device:TPU:6 before, /device:TPU:58 now
where the time goes in v2:
time: 55.8 us; the launch traced here: 55.7 us
  Pallas kernels  52.7 us (94%)
  local copies, waits for them, and re-layouts  2.32 us (4%)
  between operations  0.65 us (1%)
    pallas_call x1, Pallas kernels, body(): pl.pallas_call(functools.partial(kernel, sizes, [c.shape for c in consts]...  52.7 us
    unnamed x4, local copies, waits for them, and re-layouts  2.32 us

profile of v2, /device:TPU:58, one launch (start us, length us, event | category | flops | bytes accessed | tf_op | source)
XLA Modules:
  0.0 55.7 jit_solution(13180792252492123511)
XLA Ops:
  0.6 52.7 %sphere_steps.1 = (f32[1,16,2048]{2,1,0:T(8,128)}, f32[2,1,16,2048]{3,2,1,0:T(8,128)}) custom-call(f32[1,16,2048]{2,1,0:T(8,128)} %thick_ref.1, f32[2,1,16,2048]{3,2,1,0:T(8,128)} %wind_ref.1, bf16[256,256]{1,0:T(8,128)(2,1)} %constant.23.refs_0_, bf16[256,256]{1,0:T(8,128)(2,1)} %constant.26.refs_1_, bf16[256,256]{1,0:T(8,128)(2,1)} %constant.27.refs_2_, ...), custom_call_target="tpu_custom_call" | custom-call | tf_op jit(solution)/shard_map/sphere_steps/pallas_call | solution.py:447
  53.4 0.0 copy-start
  53.4 1.6 %copy.13 = f32[1,16,2048]{2,1,0:T(8,128)} copy(f32[1,16,2048]{2,1,0:T(8,128)} %get-tuple-element.4) | data formatting | bytes 262144
  55.0 0.0 copy-done
  55.0 0.7 %copy.14 = f32[2,1,16,2048]{3,2,1,0:T(8,128)} copy(f32[2,1,16,2048]{3,2,1,0:T(8,128)S(1)} %copy-done) | data formatting | bytes 524288
Async XLA Ops:
  53.4 1.6 %copy-start = (f32[2,1,16,2048]{3,2,1,0:T(8,128)S(1)}, f32[2,1,16,2048]{3,2,1,0:T(8,128)}, u32[]{:S(2)}) copy-start(f32[2,1,16,2048]{3,2,1,0:T(8,128)} %get-tuple-element.5) | copy-start | bytes 786436

commit v3 on v1

v3 whole, which is shorter than its diff:
```python
import functools
import math

import jax
import jax.numpy as jnp
import numpy as np
from jax import lax
from jax.experimental import pallas as pl
from jax.experimental.pallas import tpu as pltpu
from jax.sharding import PartitionSpec as P

STEPS = 2
MESH = pl.DeviceIdType.MESH

courant = 0.2
mixing = 0.25
coriolis = 0.5
cos_floor = 0.25

LANES = 128
ROWS = 8
f32 = jnp.float32
bf16 = jnp.bfloat16


def rotate(z, angle):
    re, im = z
    c, s = math.cos(angle), math.sin(angle)
    if abs(s) < 1e-12:
        return (re, im) if c > 0 else (-re, -im)
    if abs(c) < 1e-12:
        return (-im, re) if s > 0 else (im, -re)
    return re * c - im * s, re * s + im * c


def complex_sum(values, sign):
    count = len(values)
    if count == 1:
        return values
    half = count // 2
    plus = [(a[0] + b[0], a[1] + b[1]) for a, b in zip(values[:half], values[half:])]
    minus = [(a[0] - b[0], a[1] - b[1]) for a, b in zip(values[:half], values[half:])]
    minus = [rotate(z, sign * 2 * math.pi * n / count) for n, z in enumerate(minus)]
    even, odd = complex_sum(plus, sign), complex_sum(minus, sign)
    return [z for pair in zip(even, odd) for z in pair]


def odd_frequencies(values):
    count = len(values)
    if count == 1:
        return {1: (values[0], None)}
    half = count // 2
    joined = [rotate((values[n], -values[n + half]), -math.pi * n / count) for n in range(half)]
    out = {}
    for t, (re, im) in enumerate(complex_sum(joined, -1)):
        k = 4 * t + 1
        if k <= count:
            out[k] = (re, im)
        else:
            out[2 * count - k] = (re, -im)
    return out


def real_transform(values):
    count = len(values)
    if count == 1:
        return {0: (values[0], None)}
    half = count // 2
    even = real_transform([values[n] + values[n + half] for n in range(half)])
    out = {2 * k: z for k, z in even.items()}
    out.update(odd_frequencies([values[n] - values[n + half] for n in range(half)]))
    return out


def padded_transform(values):
    out = {2 * k: z for k, z in real_transform(values).items()}
    out.update(odd_frequencies(values))
    return out


def odd_inverse(terms, count):
    if count == 1:
        return [terms[1][0]]
    half = count // 2
    joined = []
    for t in range(half):
        k = 4 * t + 1
        if k <= count:
            joined.append(terms[k])
        else:
            re, im = terms[2 * count - k]
            joined.append((re, -im))
    turned = [rotate(z, math.pi * n / count) for n, z in enumerate(complex_sum(joined, 1))]
    return [z[0] for z in turned] + [-z[1] for z in turned]


def real_inverse(terms, count):
    if count == 1:
        return [terms[0][0]]
    half = count // 2
    even = real_inverse({k // 2: z for k, z in terms.items() if k % 2 == 0}, half)
    odd = odd_inverse({k: z for k, z in terms.items() if k % 2}, half)
    return [a + b for a, b in zip(even, odd)] + [a - b for a, b in zip(even, odd)]


def padded_inverse(terms, count):
    even = real_inverse({k // 2: z for k, z in terms.items() if k % 2 == 0}, count)
    odd = odd_inverse({k: z for k, z in terms.items() if k % 2}, count)
    return [a + b for a, b in zip(even, odd)]


def split(value):
    high = value.astype(bf16)
    return high, (value - high.astype(f32)).astype(bf16)


def np_split(table):
    table = jnp.asarray(table.astype(np.float32))
    high = table.astype(bf16)
    return high, (table - high.astype(f32)).astype(bf16)


def tables(lat_count):
    length = 2 * lat_count
    blocks = lat_count // LANES
    ring = 2 * blocks
    kept = length // 3
    reach = kept // ring + 1
    lane = np.arange(LANES)
    shift = np.where(lane < 2 * reach, lane - reach, 0)
    valid = (lane < 2 * reach).astype(np.float64)
    psi = 2 * np.pi * (lane[:, None] + 0.5) * shift[None, :] / LANES
    cos, sin = np.cos(psi) * valid, np.sin(psi) * valid
    forward = np.block([[cos, sin], [sin, -cos]])
    inverse = np.block([[cos.T, sin.T], [sin.T, -cos.T]])
    small = np.arange(blocks + 1)
    phi = 2 * np.pi * small[:, None] * (lane[None, :] + 0.5) / length
    twist = np.concatenate([np.cos(phi), np.sin(phi)], 1)
    index = small[:, None] + ring * shift[None, :]
    weight = np.where((small == 0) | (small == blocks), 1.0, 2.0)[:, None] / length
    weight = weight * (np.abs(index) <= kept) * valid
    slope = weight * 2 * np.pi * index / length
    factor = np.concatenate([weight, weight, slope, -slope], 1)
    latitude = (np.arange(lat_count) + 0.5) * (np.pi / lat_count) - 0.5 * np.pi
    secant = 1.0 / np.maximum(np.cos(latitude), cos_floor)
    line = np.zeros((8, lat_count))
    line[0] = secant / 60.0
    line[1] = coriolis * np.sin(latitude)
    parts = 2 * 3
    own = np.zeros((parts * ROWS, parts * ROWS))
    outer = np.zeros((parts * ROWS, parts * ROWS))
    for part in range(parts):
        for row in range(ROWS):
            for offset, value in ((1, 45.0), (2, -9.0), (3, 1.0)):
                for sign in (1, -1):
                    at = row + sign * offset
                    target = own if 0 <= at < ROWS else outer
                    target[part * ROWS + row, part * ROWS + at % ROWS] = sign * value
    own = np.concatenate([own, own], 1)
    outer = np.concatenate([outer, outer], 1)
    return (
        *np_split(forward),
        *np_split(inverse),
        jnp.asarray(twist.astype(np.float32)),
        jnp.asarray(factor.astype(np.float32)),
        jnp.asarray(line.astype(np.float32)),
        jnp.asarray(own.astype(np.float32)).astype(bf16),
        jnp.asarray(outer.astype(np.float32)).astype(bf16),
    )


def kernel(sizes, const_shapes, thick_ref, wind_ref, *refs):
    count = len(const_shapes)
    const_hbm, (out_h, out_w), scratch = refs[:count], refs[count : count + 2], refs[count + 2 :]
    const_refs, scratch = scratch[:count], scratch[count:]
    fwd_hi, fwd_lo, inv_hi, inv_lo, twist_ref, factor_ref, line_ref, own_ref, outer_ref = const_refs
    (
        state, halo, far, levels, spec_in, turned, zonal, smooth, slope, redo, const_sem, first_send, first_recv,
        far_send, far_recv, halo_send, halo_recv, lev_send, lev_recv, last_send, last_recv,
    ) = scratch
    lon_size, lev_size = sizes
    fields, _, lat_count = state.shape[1:]
    blocks = lat_count // LANES
    half = lon_size // 2
    chips = half // 2
    depth = 2 * lev_size
    lon, lev = lax.axis_index("lon"), lax.axis_index("lev")
    side_now = lon // half
    chip = (lon % half) // 2
    core = lon % 2
    odd = chip % 2
    z = side_now * lev_size + lev

    there = (z + lev_size // 2 + lev_size * ((odd + core + side_now) % 2)) % depth

    def owner(q):
        return {"lon": (there // lev_size) * half + 2 * chip + q, "lev": there % lev_size}

    place = (z + depth - lev_size // 2) % depth
    level = place % lev_size
    held_by = (place // lev_size + odd) % 2

    def holder(hemi):
        return {"lon": hemi * half + 2 * chip + held_by, "lev": level}

    across = (1 - side_now) * half + 2 * chip
    after = side_now * half + 2 * ((chip + 1) % chips)
    before = side_now * half + 2 * ((chip + chips - 1) % chips) + 1
    right = (1 - core) * (lon + 1) + core * ((1 - held_by) * across + held_by * after)
    left = core * (lon - 1) + (1 - core) * (held_by * (across + 1) + (1 - held_by) * before)
    swap_right = core * held_by * (chip // (chips - 1))
    swap_left = (1 - core) * (1 - held_by) * ((chips - 1 - chip) // (chips - 1))
    has_below, has_above = level > 0, level < lev_size - 1
    far_right, far_left = core * (1 - held_by), (1 - core) * held_by
    crossing = far_right + far_left
    beyond = (there + lev_size) % depth
    far_owner = {"lon": (beyond // lev_size) * half + 2 * chip + core, "lev": beyond % lev_size}

    def far_holder(hemi):
        return {"lon": hemi * half + 2 * chip + 1 - held_by, "lev": level}

    def at_height(height):
        return {"lon": (height // lev_size) * half + 2 * chip + core, "lev": height % lev_size}

    upward, downward = at_height((z + 1) % depth), at_height((z + depth - 1) % depth)

    loads = [pltpu.make_async_copy(const_hbm[n], const_refs[n], const_sem.at[n]) for n in range(count)]
    for copy in loads:
        copy.start()
    halo[...] = jnp.zeros_like(halo)
    far[...] = jnp.zeros_like(far)

    @pl.when(jnp.logical_not(has_below))
    def _():
        for s in range(STEPS):
            levels[s, 0] = jnp.zeros_like(levels[s, 0])

    @pl.when(jnp.logical_not(has_above))
    def _():
        for s in range(STEPS):
            levels[s, 1] = jnp.zeros_like(levels[s, 1])

    barrier = pltpu.get_barrier_semaphore()
    for device in (owner(0), owner(1), holder(0), holder(1), far_owner, {"lon": left}, {"lon": right}):
        pl.semaphore_signal(barrier, inc=1, device_id=device, device_id_type=MESH)

    @pl.when(crossing > 0)
    def _():
        for hemi in range(2):
            pl.semaphore_signal(barrier, inc=1, device_id=far_holder(hemi), device_id_type=MESH)

    @pl.when(has_below)
    def _():
        pl.semaphore_signal(barrier, inc=1, device_id=downward, device_id_type=MESH)

    @pl.when(has_above)
    def _():
        pl.semaphore_signal(barrier, inc=1, device_id=upward, device_id_type=MESH)

    def rows(part):
        return pl.ds(pl.multiple_of(part * ROWS, ROWS), ROWS)

    def first_copy(q, f, hemi):
        at = rows(q)
        return pltpu.make_async_remote_copy(
            src_ref=thick_ref.at[0, at] if f == 0 else wind_ref.at[f - 1, 0, at], dst_ref=state.at[0, f, rows(hemi)],
            send_sem=first_send.at[q, f], recv_sem=first_recv.at[hemi, f],
            device_id=owner(q), device_id_type=MESH,
        )

    def early_far_copy(f, side, hemi):
        at = pl.ds(2 * ROWS - 3 if side == 0 else 0, 3)
        return pltpu.make_async_remote_copy(
            src_ref=thick_ref.at[0, at] if f == 0 else wind_ref.at[f - 1, 0, at],
            dst_ref=far.at[0, f, hemi, pl.ds(ROWS - 3 if side == 0 else 0, 3)],
            send_sem=far_send.at[0, f, 0], recv_sem=far_recv.at[0, f, hemi],
            device_id=far_owner, device_id_type=MESH,
        )

    def last_copy(part, f, hemi, q, origin, span):
        start, length = span
        source = origin.at[f, pl.ds(hemi * ROWS + start, length)]
        at = pl.ds(q * ROWS + start, length)
        return pltpu.make_async_remote_copy(
            src_ref=source, dst_ref=out_h.at[0, at] if f == 0 else out_w.at[f - 1, 0, at],
            send_sem=last_send.at[part, hemi, f], recv_sem=last_recv.at[part, q, f],
            device_id=holder(hemi), device_id_type=MESH,
        )

    def halo_copy(s, side, f, hemi, distant=False):
        start = ROWS - 3 if side == 0 else 0
        to = hemi if distant else (hemi + (swap_right if side == 0 else swap_left)) % 2
        send, recv = far_send.at[s, f, hemi], far_recv.at[s, f, hemi]
        if not distant:
            send, recv = halo_send.at[s, side, f, hemi], halo_recv.at[s, side, f, to]
        return pltpu.make_async_remote_copy(
            src_ref=state.at[s, f, pl.ds(hemi * ROWS + start, 3)],
            dst_ref=(far if distant else halo).at[s, f, to, pl.ds(start, 3)],
            send_sem=send, recv_sem=recv,
            device_id={"lon": right if side == 0 else left}, device_id_type=MESH,
        )

    def lev_copy(s, side, hemi):
        return pltpu.make_async_remote_copy(
            src_ref=state.at[s, 0, rows(hemi)], dst_ref=levels.at[s, side, rows(hemi)],
            send_sem=lev_send.at[s, side, hemi], recv_sem=lev_recv.at[s, side, hemi],
            device_id=upward if side == 0 else downward, device_id_type=MESH,
        )

    whole, spans = (0, ROWS), {0: ((0, ROWS - 3), (ROWS - 3, 3)), 1: ((3, ROWS - 3), (0, 3))}

    def if_far(action):
        for side, flag in ((0, far_right), (1, far_left)):

            @pl.when(flag > 0)
            def _(side=side):
                action(side)

    def send_halo(s, hemi, chosen):
        def distant(side):
            for f in chosen:
                halo_copy(s, side, f, hemi, True).start()

        if s > 0:
            if_far(distant)
        for side, flag in ((0, far_right), (1, far_left)):

            @pl.when(flag == 0)
            def _(side=side):
                for f in chosen:
                    halo_copy(s, side, f, hemi).start()

    def near_halo(s, wait):
        for side, flag in ((0, far_left), (1, far_right)) if wait == "wait_recv" else ((0, far_right), (1, far_left)):

            @pl.when(flag == 0)
            def _(side=side):
                for f in range(fields):
                    for hemi in range(2):
                        getattr(halo_copy(s, side, f, hemi), wait)()

    def far_wait(s):
        for f in range(fields):
            for hemi in range(2):
                halo_copy(s, 1, f, hemi, True).wait_recv()

    def each_level(s, hemi, action):
        for side, flags in ((0, (has_above, has_below)), (1, (has_below, has_above))):

            @pl.when(flags[1 if action == "wait_recv" else 0])
            def _(side=side):
                getattr(lev_copy(s, side, hemi), action)()

    def product(value, high, low):
        top, rest = split(value)
        out = jnp.dot(top, low[...], preferred_element_type=f32)
        out += jnp.dot(rest, high[...], preferred_element_type=f32)
        return out + jnp.dot(top, high[...], preferred_element_type=f32)

    spectral = (blocks + 1) * 2 * ROWS

    def spectra(s, f):
        for hemi in range(2):
            r = slice(hemi * ROWS, (hemi + 1) * ROWS)
            values = [state[s, f, r, n * LANES : (n + 1) * LANES] for n in range(blocks)]
            for k, (re, im) in padded_transform(values).items():
                at = (2 * k + hemi) * ROWS
                c, d = twist_ref[k : k + 1, :LANES], twist_ref[k : k + 1, LANES:]
                if k == 0:
                    out = (re, jnp.zeros_like(re))
                elif im is None:
                    out = (re * c, -re * d)
                else:
                    out = (re * c + im * d, im * c - re * d)
                spec_in[at : at + ROWS, :LANES] = out[0]
                spec_in[at : at + ROWS, LANES:] = out[1]
        gains = product(spec_in[...], fwd_hi, fwd_lo)
        sign = 1.0 if f == 0 else -1.0
        for k in range(blocks + 1):
            at = 2 * k * ROWS
            to = at + ROWS
            end = to + ROWS
            a = gains[at:to, :LANES] + sign * gains[to:end, :LANES]
            b = gains[at:to, LANES:] - sign * gains[to:end, LANES:]
            w = factor_ref[k : k + 1]
            pieces = (a * w[:, :LANES], b * w[:, LANES : 2 * LANES])
            turned[at:to, :LANES] = pieces[0]
            turned[at:to, LANES:] = pieces[1]
            turned[to:end, :LANES] = sign * pieces[0]
            turned[to:end, LANES:] = -sign * pieces[1]
            at, to, end = at + spectral, to + spectral, end + spectral
            pieces = (b * w[:, 2 * LANES : 3 * LANES], a * w[:, 3 * LANES :])
            turned[at:to, :LANES] = pieces[0]
            turned[at:to, LANES:] = pieces[1]
            turned[to:end, :LANES] = -sign * pieces[0]
            turned[to:end, LANES:] = sign * pieces[1]
        turned[...] = product(turned[...], inv_hi, inv_lo)
        for which, target in enumerate((smooth, slope)):
            for hemi in range(2):
                terms = {}
                for k in range(blocks + 1):
                    at = which * spectral + (2 * k + hemi) * ROWS
                    re, im = turned[at : at + ROWS, :LANES], turned[at : at + ROWS, LANES:]
                    c, d = twist_ref[k : k + 1, :LANES], twist_ref[k : k + 1, LANES:]
                    if k == 0:
                        terms[k] = (re, None)
                    elif k == blocks:
                        terms[k] = (re * c - im * d, None)
                    else:
                        terms[k] = (re * c - im * d, re * d + im * c)
                r = slice(hemi * ROWS, (hemi + 1) * ROWS)
                for n, value in enumerate(padded_inverse(terms, blocks)):
                    target[f, r, n * LANES : (n + 1) * LANES] = value

    def own_zonal(s):
        value = state[s].reshape(fields * 2 * ROWS, lat_count)
        zonal[...] = jnp.dot(own_ref[...], jnp.concatenate(split(value), 0), preferred_element_type=f32)

    def outer_zonal(value):
        value = value.reshape(fields * 2 * ROWS, lat_count)
        zonal[...] += jnp.dot(outer_ref[...], jnp.concatenate(split(value), 0), preferred_element_type=f32)

    def advance(s, hemi, target):
        r = slice(hemi * ROWS, (hemi + 1) * ROWS)
        for n in range(blocks):
            lanes = slice(n * LANES, (n + 1) * LANES)
            h, u, v = (state[s, f, r, lanes] for f in range(fields))
            secant, turn = line_ref[0:1, lanes], line_ref[1:2, lanes]
            zh, zu, zv = (
                zonal[(2 * f + hemi) * ROWS : (2 * f + hemi + 1) * ROWS, lanes] * secant for f in range(fields)
            )
            mh, mu, mv = (slope[f, r, lanes] for f in range(fields))
            vertical = levels[s, 0, r, lanes] + levels[s, 1, r, lanes] - 2.0 * h
            th = mixing * vertical - (u * zh + v * mh) - h * (zu + mv)
            tu = turn * v - (u * zu + v * mu) - zh
            tv = -(u * zv + v * mv) - mh - turn * u
            for f, t in enumerate((th, tu, tv)):
                target[f, r, lanes] = smooth[f, r, lanes] + courant * t

    count_here = 7 + 2 * crossing + has_below.astype(jnp.int32) + has_above.astype(jnp.int32)
    pl.semaphore_wait(barrier, count_here)
    for f in range(fields):
        for q in range(2):
            first_copy(q, f, side_now).start()
        for side in range(2):

            @pl.when(core == side)
            def _(side=side):
                early_far_copy(f, side, side_now).start()

    for copy in loads:
        copy.wait()
    for s in range(STEPS):
        for f in range(fields):
            if s == 0:
                for hemi in range(2):
                    first_copy(core, f, hemi).wait_recv()
                    if f == 0:
                        each_level(0, hemi, "start")
                    send_halo(0, hemi, (f,))
            spectra(s, f)
        own_zonal(s)
        near_halo(s, "wait_recv")
        if s < STEPS - 1:

            @pl.when(crossing > 0)
            def _():
                far_wait(s)

            outer_zonal(halo[s] + far[s])
        else:
            outer_zonal(halo[s])
        for hemi in range(2):
            each_level(s, hemi, "wait_recv")
            target = state.at[s + 1]
            advance(s, hemi, target)
            if s < STEPS - 1:
                send_halo(s + 1, hemi, range(fields))
                each_level(s + 1, hemi, "start")
                continue

            @pl.when(crossing == 0)
            def _(hemi=hemi):
                for f in range(fields):
                    last_copy(0, f, hemi, core, target, whole).start()

            @if_far
            def _(side, hemi=hemi):
                for f in range(fields):
                    last_copy(0, f, hemi, 1 - side, target, spans[side][0]).start()

    @pl.when(crossing > 0)
    def _():
        far_wait(STEPS - 1)
        outer_zonal(far[STEPS - 1])
        for hemi in range(2):
            advance(STEPS - 1, hemi, redo)

            @if_far
            def _(side, hemi=hemi):
                for f in range(fields):
                    last_copy(1, f, hemi, 1 - side, redo, spans[side][1]).start()

    target = state.at[STEPS]
    for side in range(2):

        @pl.when(core == side)
        def _(side=side):
            for f in range(fields):
                last_copy(0, f, 0, side, target, whole).wait_recv()
                last_copy(0, f, 0, 1 - side, target, spans[side][0]).wait_recv()
                last_copy(1, f, 0, 1 - side, redo, spans[side][1]).wait_recv()

    for f in range(fields):
        for q in range(2):
            first_copy(q, f, side_now).wait_send()
        early_far_copy(f, 0, side_now).wait_send()
    for hemi in range(2):

        @pl.when(crossing == 0)
        def _(hemi=hemi):
            for f in range(fields):
                last_copy(0, f, hemi, core, target, whole).wait_send()

        @if_far
        def _(side, hemi=hemi):
            for f in range(fields):
                for s in range(1, STEPS):
                    halo_copy(s, side, f, hemi, True).wait_send()
                last_copy(0, f, hemi, 1 - side, target, spans[side][0]).wait_send()
                last_copy(1, f, hemi, 1 - side, redo, spans[side][1]).wait_send()

        for s in range(STEPS):
            each_level(s, hemi, "wait_send")
    for s in range(STEPS):
        near_halo(s, "wait_send")


def body(sizes, thickness, wind_field):
    level_count, lon_count, lat_count = thickness.shape
    fields = 3
    blocks = lat_count // LANES
    spectral = (blocks + 1) * 2 * ROWS
    consts = tables(lat_count)
    hbm = pl.BlockSpec(memory_space=pltpu.HBM)
    dma = pltpu.SemaphoreType.DMA
    return pl.pallas_call(
        functools.partial(kernel, sizes, [c.shape for c in consts]),
        out_shape=(
            jax.ShapeDtypeStruct(thickness.shape, f32),
            jax.ShapeDtypeStruct(wind_field.shape, f32),
        ),
        in_specs=[hbm, hbm] + [hbm] * len(consts),
        out_specs=(hbm, hbm),
        scratch_shapes=[pltpu.VMEM(c.shape, c.dtype) for c in consts]
        + [
            pltpu.VMEM((STEPS + 1, fields, lon_count, lat_count), f32),
            pltpu.VMEM((STEPS, fields, 2, ROWS, lat_count), f32),
            pltpu.VMEM((STEPS, fields, 2, ROWS, lat_count), f32),
            pltpu.VMEM((STEPS, 2, lon_count, lat_count), f32),
            pltpu.VMEM((spectral, 2 * LANES), f32),
            pltpu.VMEM((2 * spectral, 2 * LANES), f32),
            pltpu.VMEM((fields * lon_count, lat_count), f32),
            pltpu.VMEM((fields, lon_count, lat_count), f32),
            pltpu.VMEM((fields, lon_count, lat_count), f32),
            pltpu.VMEM((fields, lon_count, lat_count), f32),
            dma((len(consts),)),
            dma((2, fields)),
            dma((2, fields)),
            dma((STEPS, fields, 2)),
            dma((STEPS, fields, 2)),
            dma((STEPS, 2, fields, 2)),
            dma((STEPS, 2, fields, 2)),
            dma((STEPS, 2, 2)),
            dma((STEPS, 2, 2)),
            dma((2, 2, fields)),
            dma((2, 2, fields)),
        ],
        name="sphere_steps",
        compiler_params=pltpu.CompilerParams(collective_id=0, has_side_effects=True, vmem_limit_bytes=67_043_328),
    )(thickness, wind_field, *consts)


def solution(mesh):
    sizes = (mesh.shape["lon"], mesh.shape["lev"])
    in_specs = (P("lev", "lon", None), P(None, "lev", "lon", None))
    out_specs = (P("lev", "lon", None), P(None, "lev", "lon", None))
    return jax.shard_map(
        functools.partial(body, sizes), mesh=mesh, in_specs=in_specs, out_specs=out_specs, check_vma=False
    )
```

time: 67.9 us -> 49.1 us (0.72)
  the two profiles are of different devices: /device:TPU:6 before, /device:TPU:23 now
where the time goes in v3:
time: 49.1 us; the launch traced here: 48.9 us
  Pallas kernels  46 us (94%)
  local copies, waits for them, and re-layouts  2.32 us (5%)
  between operations  0.65 us (1%)
    pallas_call x1, Pallas kernels, body(): pl.pallas_call(functools.partial(kernel, sizes, [c.shape for c in consts]...  46 us
    unnamed x4, local copies, waits for them, and re-layouts  2.32 us

profile of v3, /device:TPU:23, one launch (start us, length us, event | category | flops | bytes accessed | tf_op | source)
XLA Modules:
  0.0 48.9 jit_solution(4663708397384351456)
XLA Ops:
  0.6 46.0 %sphere_steps.1 = (f32[1,16,2048]{2,1,0:T(8,128)}, f32[2,1,16,2048]{3,2,1,0:T(8,128)}) custom-call(f32[1,16,2048]{2,1,0:T(8,128)} %thick_ref.1, f32[2,1,16,2048]{3,2,1,0:T(8,128)} %wind_ref.1, bf16[256,256]{1,0:T(8,128)(2,1)} %constant.23.refs_0_, bf16[256,256]{1,0:T(8,128)(2,1)} %constant.26.refs_1_, bf16[256,256]{1,0:T(8,128)(2,1)} %constant.27.refs_2_, ...), custom_call_target="tpu_custom_call" | custom-call | tf_op jit(solution)/shard_map/sphere_steps/pallas_call | solution.py:547
  46.6 0.0 copy-start
  46.6 1.6 %copy.13 = f32[1,16,2048]{2,1,0:T(8,128)} copy(f32[1,16,2048]{2,1,0:T(8,128)} %get-tuple-element.4) | data formatting | bytes 262144
  48.2 0.0 copy-done
  48.2 0.7 %copy.14 = f32[2,1,16,2048]{3,2,1,0:T(8,128)} copy(f32[2,1,16,2048]{3,2,1,0:T(8,128)S(1)} %copy-done) | data formatting | bytes 524288
Async XLA Ops:
  46.6 1.6 %copy-start = (f32[2,1,16,2048]{3,2,1,0:T(8,128)S(1)}, f32[2,1,16,2048]{3,2,1,0:T(8,128)}, u32[]{:S(2)}) copy-start(f32[2,1,16,2048]{3,2,1,0:T(8,128)} %get-tuple-element.5) | copy-start | bytes 786436

commit v4 on v3

--- a/solution.py
+++ b/solution.py
@@ -241,8 +241,14 @@
             levels[s, 1] = jnp.zeros_like(levels[s, 1])
 
     barrier = pltpu.get_barrier_semaphore()
-    for device in (owner(0), owner(1), holder(0), holder(1), far_owner, {"lon": left}, {"lon": right}):
+    for device in (owner(0), owner(1), holder(0), holder(1), far_owner):
         pl.semaphore_signal(barrier, inc=1, device_id=device, device_id_type=MESH)
+
+    for at, flag in ((left, far_left), (right, far_right)):
+
+        @pl.when(flag == 0)
+        def _(at=at):
+            pl.semaphore_signal(barrier, inc=1, device_id={"lon": at}, device_id_type=MESH)
 
     @pl.when(crossing > 0)
     def _():
@@ -316,13 +322,14 @@
             def _(side=side):
                 action(side)
 
+    def send_far(s):
+        @if_far
+        def _(side):
+            for hemi in range(2):
+                for f in range(fields):
+                    halo_copy(s, side, f, hemi, True).start()
+
     def send_halo(s, hemi, chosen):
-        def distant(side):
-            for f in chosen:
-                halo_copy(s, side, f, hemi, True).start()
-
-        if s > 0:
-            if_far(distant)
         for side, flag in ((0, far_right), (1, far_left)):
 
             @pl.when(flag == 0)
@@ -437,7 +444,7 @@
             for f, t in enumerate((th, tu, tv)):
                 target[f, r, lanes] = smooth[f, r, lanes] + courant * t
 
-    count_here = 7 + 2 * crossing + has_below.astype(jnp.int32) + has_above.astype(jnp.int32)
+    count_here = 7 + crossing + has_below.astype(jnp.int32) + has_above.astype(jnp.int32)
     pl.semaphore_wait(barrier, count_here)
     for f in range(fields):
         for q in range(2):
@@ -477,6 +484,8 @@
             if s < STEPS - 1:
                 send_halo(s + 1, hemi, range(fields))
                 each_level(s + 1, hemi, "start")
+                if hemi == 1:
+                    send_far(s + 1)
                 continue
 
             @pl.when(crossing == 0)
@@ -543,15 +552,16 @@
     spectral = (blocks + 1) * 2 * ROWS
     consts = tables(lat_count)
     hbm = pl.BlockSpec(memory_space=pltpu.HBM)
+    vmem = pl.BlockSpec(memory_space=pltpu.VMEM)
     dma = pltpu.SemaphoreType.DMA
     return pl.pallas_call(
         functools.partial(kernel, sizes, [c.shape for c in consts]),
         out_shape=(
-            jax.ShapeDtypeStruct(thickness.shape, f32),
-            jax.ShapeDtypeStruct(wind_field.shape, f32),
+            pltpu.VMEM(thickness.shape, f32),
+            pltpu.VMEM(wind_field.shape, f32),
         ),
         in_specs=[hbm, hbm] + [hbm] * len(consts),
-        out_specs=(hbm, hbm),
+        out_specs=(vmem, vmem),
         scratch_shapes=[pltpu.VMEM(c.shape, c.dtype) for c in consts]
         + [
             pltpu.VMEM((STEPS + 1, fields, lon_count, lat_count), f32),
@@ -577,7 +587,7 @@
             dma((2, 2, fields)),
         ],
         name="sphere_steps",
-        compiler_params=pltpu.CompilerParams(collective_id=0, has_side_effects=True, vmem_limit_bytes=67_043_328),
+        compiler_params=pltpu.CompilerParams(collective_id=0, has_side_effects=True, vmem_limit_bytes=66_200_000),
     )(thickness, wind_field, *consts)
 
 

time: 49.1 us -> 48.6 us (0.990)
  the two profiles are of different devices: /device:TPU:23 before, /device:TPU:39 now
where the time goes in v4:
time: 48.6 us; the launch traced here: 48.5 us
  Pallas kernels  46.5 us (96%)
  local copies, waits for them, and re-layouts  1.36 us (3%)
  between operations  0.64 us (1%)
    pallas_call x1, Pallas kernels, body(): pl.pallas_call(functools.partial(kernel, sizes, [c.shape for c in consts]...  46.5 us
    unnamed x2, local copies, waits for them, and re-layouts  1.36 us

profile of v4, /device:TPU:39, one launch (start us, length us, event | category | flops | bytes accessed | tf_op | source)
XLA Modules:
  0.0 48.5 jit_solution(12789096863647180333)
XLA Ops:
  0.6 46.5 %sphere_steps.1 = (f32[1,16,2048]{2,1,0:T(8,128)S(1)}, f32[2,1,16,2048]{3,2,1,0:T(8,128)S(1)}) custom-call(f32[1,16,2048]{2,1,0:T(8,128)} %thick_ref.1, f32[2,1,16,2048]{3,2,1,0:T(8,128)} %wind_ref.1, bf16[256,256]{1,0:T(8,128)(2,1)} %constant.23.refs_0_, bf16[256,256]{1,0:T(8,128)(2,1)} %constant.26.refs_1_, bf16[256,256]{1,0:T(8,128)(2,1)} %constant.27.refs_2_, ...), custom_call_target="tpu_custom_call" | custom-call | tf_op jit(solution)/shard_map/sphere_steps/pallas_call | solution.py:557
  47.1 0.7 %copy.13 = f32[1,16,2048]{2,1,0:T(8,128)} copy(f32[1,16,2048]{2,1,0:T(8,128)S(1)} %get-tuple-element.2) | data formatting | bytes 262144
  47.8 0.7 %copy.14 = f32[2,1,16,2048]{3,2,1,0:T(8,128)} copy(f32[2,1,16,2048]{3,2,1,0:T(8,128)S(1)} %get-tuple-element.3) | data formatting | bytes 524288

commit v5 on v4

--- a/solution.py
+++ b/solution.py
@@ -322,12 +322,11 @@
             def _(side=side):
                 action(side)
 
-    def send_far(s):
+    def send_far(s, hemi):
         @if_far
         def _(side):
-            for hemi in range(2):
-                for f in range(fields):
-                    halo_copy(s, side, f, hemi, True).start()
+            for f in range(fields):
+                halo_copy(s, side, f, hemi, True).start()
 
     def send_halo(s, hemi, chosen):
         for side, flag in ((0, far_right), (1, far_left)):
@@ -482,10 +481,9 @@
             target = state.at[s + 1]
             advance(s, hemi, target)
             if s < STEPS - 1:
+                send_far(s + 1, hemi)
                 send_halo(s + 1, hemi, range(fields))
                 each_level(s + 1, hemi, "start")
-                if hemi == 1:
-                    send_far(s + 1)
                 continue
 
             @pl.when(crossing == 0)

time: 48.6 us -> 46.3 us (0.953)
  the two profiles are of different devices: /device:TPU:39 before, /device:TPU:1 now
where the time goes in v5:
time: 46.3 us; the launch traced here: 46.2 us
  Pallas kernels  44.2 us (95%)
  local copies, waits for them, and re-layouts  1.36 us (3%)
  between operations  0.64 us (1%)
    pallas_call x1, Pallas kernels, body(): pl.pallas_call(functools.partial(kernel, sizes, [c.shape for c in consts]...  44.2 us
    unnamed x2, local copies, waits for them, and re-layouts  1.36 us

profile of v5, /device:TPU:1, one launch (start us, length us, event | category | flops | bytes accessed | tf_op | source)
XLA Modules:
  0.0 46.2 jit_solution(16516065009777311124)
XLA Ops:
  0.6 44.2 %sphere_steps.1 = (f32[1,16,2048]{2,1,0:T(8,128)S(1)}, f32[2,1,16,2048]{3,2,1,0:T(8,128)S(1)}) custom-call(f32[1,16,2048]{2,1,0:T(8,128)} %thick_ref.1, f32[2,1,16,2048]{3,2,1,0:T(8,128)} %wind_ref.1, bf16[256,256]{1,0:T(8,128)(2,1)} %constant.23.refs_0_, bf16[256,256]{1,0:T(8,128)(2,1)} %constant.26.refs_1_, bf16[256,256]{1,0:T(8,128)(2,1)} %constant.27.refs_2_, ...), custom_call_target="tpu_custom_call" | custom-call | tf_op jit(solution)/shard_map/sphere_steps/pallas_call | solution.py:555
  44.9 0.7 %copy.13 = f32[1,16,2048]{2,1,0:T(8,128)} copy(f32[1,16,2048]{2,1,0:T(8,128)S(1)} %get-tuple-element.2) | data formatting | bytes 262144
  45.5 0.7 %copy.14 = f32[2,1,16,2048]{3,2,1,0:T(8,128)} copy(f32[2,1,16,2048]{3,2,1,0:T(8,128)S(1)} %get-tuple-element.3) | data formatting | bytes 524288

commit v6 on v5

--- a/solution.py
+++ b/solution.py
@@ -335,6 +335,14 @@
             def _(side=side):
                 for f in chosen:
                     halo_copy(s, side, f, hemi).start()
+
+    def send_early_far():
+        for side in range(2):
+
+            @pl.when(core == side)
+            def _(side=side):
+                for f in range(fields):
+                    early_far_copy(f, side, side_now).start()
 
     def near_halo(s, wait):
         for side, flag in ((0, far_left), (1, far_right)) if wait == "wait_recv" else ((0, far_right), (1, far_left)):
@@ -448,11 +456,6 @@
     for f in range(fields):
         for q in range(2):
             first_copy(q, f, side_now).start()
-        for side in range(2):
-
-            @pl.when(core == side)
-            def _(side=side):
-                early_far_copy(f, side, side_now).start()
 
     for copy in loads:
         copy.wait()
@@ -461,9 +464,12 @@
             if s == 0:
                 for hemi in range(2):
                     first_copy(core, f, hemi).wait_recv()
-                    if f == 0:
+                    send_halo(0, hemi, (f,))
+                if f == fields - 2:
+                    send_early_far()
+                if f == fields - 1:
+                    for hemi in range(2):
                         each_level(0, hemi, "start")
-                    send_halo(0, hemi, (f,))
             spectra(s, f)
         own_zonal(s)
         near_halo(s, "wait_recv")

time: 46.3 us -> 49.1 us (1.060)
  Pallas kernels: 44.2 us -> 47 us
    pallas_call x1, Pallas kernels: 44.2 us -> 47 us  [body(): pl.pallas_call(functools.partial(kernel, sizes, [c.shape for c in consts]...]
where the time goes in v6:
time: 49.1 us; the launch traced here: 49 us
  Pallas kernels  47 us (96%)
  local copies, waits for them, and re-layouts  1.36 us (3%)
  between operations  0.64 us (1%)
    pallas_call x1, Pallas kernels, body(): pl.pallas_call(functools.partial(kernel, sizes, [c.shape for c in consts]...  47 us
    unnamed x2, local copies, waits for them, and re-layouts  1.36 us

profile of v6, /device:TPU:1, one launch (start us, length us, event | category | flops | bytes accessed | tf_op | source)
XLA Modules:
  0.0 49.0 jit_solution(14797494989735864356)
XLA Ops:
  0.6 47.0 %sphere_steps.1 = (f32[1,16,2048]{2,1,0:T(8,128)S(1)}, f32[2,1,16,2048]{3,2,1,0:T(8,128)S(1)}) custom-call(f32[1,16,2048]{2,1,0:T(8,128)} %thick_ref.1, f32[2,1,16,2048]{3,2,1,0:T(8,128)} %wind_ref.1, bf16[256,256]{1,0:T(8,128)(2,1)} %constant.23.refs_0_, bf16[256,256]{1,0:T(8,128)(2,1)} %constant.26.refs_1_, bf16[256,256]{1,0:T(8,128)(2,1)} %constant.27.refs_2_, ...), custom_call_target="tpu_custom_call" | custom-call | tf_op jit(solution)/shard_map/sphere_steps/pallas_call | solution.py:561
  47.7 0.7 %copy.13 = f32[1,16,2048]{2,1,0:T(8,128)} copy(f32[1,16,2048]{2,1,0:T(8,128)S(1)} %get-tuple-element.2) | data formatting | bytes 262144
  48.3 0.7 %copy.14 = f32[2,1,16,2048]{3,2,1,0:T(8,128)} copy(f32[2,1,16,2048]{3,2,1,0:T(8,128)S(1)} %get-tuple-element.3) | data formatting | bytes 524288

commit v7 on v5

--- a/solution.py
+++ b/solution.py
@@ -175,7 +175,7 @@
     const_refs, scratch = scratch[:count], scratch[count:]
     fwd_hi, fwd_lo, inv_hi, inv_lo, twist_ref, factor_ref, line_ref, own_ref, outer_ref = const_refs
     (
-        state, halo, far, levels, spec_in, turned, zonal, smooth, slope, redo, const_sem, first_send, first_recv,
+        state, halo, far, levels, spec_in, turned, zonal, smooth, slope, redo, ahead, const_sem, first_send, first_recv,
         far_send, far_recv, halo_send, halo_recv, lev_send, lev_recv, last_send, last_recv,
     ) = scratch
     lon_size, lev_size = sizes
@@ -300,7 +300,7 @@
         if not distant:
             send, recv = halo_send.at[s, side, f, hemi], halo_recv.at[s, side, f, to]
         return pltpu.make_async_remote_copy(
-            src_ref=state.at[s, f, pl.ds(hemi * ROWS + start, 3)],
+            src_ref=(ahead.at[max(s - 1, 0)] if distant else state.at[s]).at[f, pl.ds(hemi * ROWS + start, 3)],
             dst_ref=(far if distant else halo).at[s, f, to, pl.ds(start, 3)],
             send_sem=send, recv_sem=recv,
             device_id={"lon": right if side == 0 else left}, device_id_type=MESH,
@@ -466,22 +466,26 @@
                     send_halo(0, hemi, (f,))
             spectra(s, f)
         own_zonal(s)
-        near_halo(s, "wait_recv")
         if s < STEPS - 1:
+            for hemi in range(2):
+                each_level(s, hemi, "wait_recv")
 
             @pl.when(crossing > 0)
             def _():
                 far_wait(s)
-
-            outer_zonal(halo[s] + far[s])
-        else:
-            outer_zonal(halo[s])
+                outer_zonal(far[s])
+                for hemi in range(2):
+                    advance(s, hemi, ahead.at[s])
+                    send_far(s + 1, hemi)
+
+        near_halo(s, "wait_recv")
+        outer_zonal(halo[s])
         for hemi in range(2):
-            each_level(s, hemi, "wait_recv")
+            if s == STEPS - 1:
+                each_level(s, hemi, "wait_recv")
             target = state.at[s + 1]
             advance(s, hemi, target)
             if s < STEPS - 1:
-                send_far(s + 1, hemi)
                 send_halo(s + 1, hemi, range(fields))
                 each_level(s + 1, hemi, "start")
                 continue
@@ -572,6 +576,7 @@
             pltpu.VMEM((fields, lon_count, lat_count), f32),
             pltpu.VMEM((fields, lon_count, lat_count), f32),
             pltpu.VMEM((fields, lon_count, lat_count), f32),
+            pltpu.VMEM((STEPS - 1, fields, lon_count, lat_count), f32),
             dma((len(consts),)),
             dma((2, fields)),
             dma((2, fields)),

time: 46.3 us -> 46.9 us (1.013)
  no operation moved by 1% of the time
where the time goes in v7:
time: 46.9 us; the launch traced here: 46.5 us
  Pallas kernels  44.5 us (95%)
  local copies, waits for them, and re-layouts  1.36 us (3%)
  between operations  0.64 us (1%)
    pallas_call x1, Pallas kernels, body(): pl.pallas_call(functools.partial(kernel, sizes, [c.shape for c in consts]...  44.5 us
    unnamed x2, local copies, waits for them, and re-layouts  1.36 us

profile of v7, /device:TPU:1, one launch (start us, length us, event | category | flops | bytes accessed | tf_op | source)
XLA Modules:
  0.0 46.5 jit_solution(9676801267751311188)
XLA Ops:
  0.6 44.5 %sphere_steps.1 = (f32[1,16,2048]{2,1,0:T(8,128)S(1)}, f32[2,1,16,2048]{3,2,1,0:T(8,128)S(1)}) custom-call(f32[1,16,2048]{2,1,0:T(8,128)} %thick_ref.1, f32[2,1,16,2048]{3,2,1,0:T(8,128)} %wind_ref.1, bf16[256,256]{1,0:T(8,128)(2,1)} %constant.23.refs_0_, bf16[256,256]{1,0:T(8,128)(2,1)} %constant.26.refs_1_, bf16[256,256]{1,0:T(8,128)(2,1)} %constant.27.refs_2_, ...), custom_call_target="tpu_custom_call" | custom-call | tf_op jit(solution)/shard_map/sphere_steps/pallas_call | solution.py:559
  45.1 0.7 %copy.13 = f32[1,16,2048]{2,1,0:T(8,128)} copy(f32[1,16,2048]{2,1,0:T(8,128)S(1)} %get-tuple-element.2) | data formatting | bytes 262144
  45.8 0.7 %copy.14 = f32[2,1,16,2048]{3,2,1,0:T(8,128)} copy(f32[2,1,16,2048]{3,2,1,0:T(8,128)S(1)} %get-tuple-element.3) | data formatting | bytes 524288

commit v8 on v7

--- a/solution.py
+++ b/solution.py
@@ -486,8 +486,8 @@
             target = state.at[s + 1]
             advance(s, hemi, target)
             if s < STEPS - 1:
+                each_level(s + 1, hemi, "start")
                 send_halo(s + 1, hemi, range(fields))
-                each_level(s + 1, hemi, "start")
                 continue
 
             @pl.when(crossing == 0)

time: 46.9 us -> 46.9 us (level)
  no operation moved by 1% of the time
where the time goes in v8:
time: 46.9 us; the launch traced here: 46.5 us
  Pallas kernels  44.5 us (95%)
  local copies, waits for them, and re-layouts  1.36 us (3%)
  between operations  0.64 us (1%)
    pallas_call x1, Pallas kernels, body(): pl.pallas_call(functools.partial(kernel, sizes, [c.shape for c in consts]...  44.5 us
    unnamed x2, local copies, waits for them, and re-layouts  1.36 us

profile of v8, /device:TPU:1, one launch (start us, length us, event | category | flops | bytes accessed | tf_op | source)
XLA Modules:
  0.0 46.5 jit_solution(585611875159292791)
XLA Ops:
  0.6 44.5 %sphere_steps.1 = (f32[1,16,2048]{2,1,0:T(8,128)S(1)}, f32[2,1,16,2048]{3,2,1,0:T(8,128)S(1)}) custom-call(f32[1,16,2048]{2,1,0:T(8,128)} %thick_ref.1, f32[2,1,16,2048]{3,2,1,0:T(8,128)} %wind_ref.1, bf16[256,256]{1,0:T(8,128)(2,1)} %constant.23.refs_0_, bf16[256,256]{1,0:T(8,128)(2,1)} %constant.26.refs_1_, bf16[256,256]{1,0:T(8,128)(2,1)} %constant.27.refs_2_, ...), custom_call_target="tpu_custom_call" | custom-call | tf_op jit(solution)/shard_map/sphere_steps/pallas_call | solution.py:559
  45.1 0.7 %copy.13 = f32[1,16,2048]{2,1,0:T(8,128)} copy(f32[1,16,2048]{2,1,0:T(8,128)S(1)} %get-tuple-element.2) | data formatting | bytes 262144
  45.8 0.7 %copy.14 = f32[2,1,16,2048]{3,2,1,0:T(8,128)} copy(f32[2,1,16,2048]{3,2,1,0:T(8,128)S(1)} %get-tuple-element.3) | data formatting | bytes 524288
